TPU v7x, 32 devices: a whole 2x2x4 slice. The times are simulated.
32 devices in a mesh: shot: 2 (over y), gx: 4 (over z), gy: 4 (over x, core).
Axes of the slice: x: 2, y: 2, z: 4, core: 2. Of those that a mesh axis runs over, the one named last changes fastest.
Arguments:
- source_prev: float32 [64, 32, 320], P(('shot', 'gx'), 'gy'), parts along dimension 0, may hold values from -0.6 to 0.6
- source_now: float32 [64, 32, 320], P(('shot', 'gx'), 'gy'), parts along dimension 0, may hold values from -0.6 to 0.6
- receiver_prev: float32 [64, 32, 320], P(('shot', 'gx'), 'gy'), parts along dimension 0, may hold values from -6 to 6
- receiver_now: float32 [64, 32, 320], P(('shot', 'gx'), 'gy'), parts along dimension 0, may hold values from -6 to 6
- speed_squared: float32 [64, 32, 320], P(('shot', 'gx'), 'gy'), parts along dimension 0, may hold values from 0.05 to 0.18
- wavelet: float32 [20], P('shot'), parts along dimension 0, may hold values from -40 to 40
- source_cell: int32 [2], P('shot'), parts along dimension 0, may hold values from 0 to 327679
- traces: float32 [20, 1024], P('shot', ('gx', 'gy')), parts along dimension 0, may hold values from -18 to 18
- receiver_cells: int32 [2, 1024], P('shot', ('gx', 'gy')), parts along dimension 0, may hold values from 0 to 1023
- plan: int32 [8], P('shot'), parts along dimension 0, may hold values from 0 to 9, as said below
- stored_snapshots: bfloat16 [8, 32, 32, 320], P('shot', 'gx', 'gy'), parts along dimension 0, may hold values from -6 to 6
- image_before: float32 [64, 32, 320], P(('shot', 'gx'), 'gy'), parts along dimension 0, may hold values from -6 to 6
Outputs:
- new_source_prev: float32 [64, 32, 320], P(('shot', 'gx'), 'gy'), parts along dimension 0
- new_source_now: float32 [64, 32, 320], P(('shot', 'gx'), 'gy'), parts along dimension 0
- new_receiver_prev: float32 [64, 32, 320], P(('shot', 'gx'), 'gy'), parts along dimension 0
- new_receiver_now: float32 [64, 32, 320], P(('shot', 'gx'), 'gy'), parts along dimension 0
- snapshots: bfloat16 [8, 32, 32, 320], P('shot', 'gx', 'gy'), parts along dimension 0
- image: float32 [64, 32, 320], P(('shot', 'gx'), 'gy'), parts along dimension 0
There are 2 independent parts, one for each index of `shot`. A program takes and returns all parts, laid end to end along the dimension named above; each array names one. Nothing has to cross between parts.
Inputs may be any that keep to these rules, and one draw needn't show every extreme that they name: `plan`: 4 different steps in increasing order; the first is 0 and the last is 9.
All inputs are finite; a program needn't handle non-finite values.
Results may differ from a plain program's by a relative error of at most 0.001.
Values sent between devices are 32-bit elements; how exact they have to be, the bound alone decides.
A program may use at most 64 MiB of HBM per device.

v0:
```python
import jax
import jax.numpy as jnp
from jax import lax
from jax.sharding import PartitionSpec as P

STENCIL_COEFFS = (-205.0 / 72.0, 8.0 / 5.0, -1.0 / 5.0, 8.0 / 315.0, -1.0 / 560.0)


def with_halo(block, sides, width):
    for axis, dim in sides:
        count = lax.axis_size(axis)
        forward = [(i, i + 1) for i in range(count - 1)]
        backward = [(target, source) for source, target in forward]
        low = lax.ppermute(
            lax.slice_in_dim(block, block.shape[dim] - width, None, axis=dim), axis, forward
        )
        high = lax.ppermute(lax.slice_in_dim(block, 0, width, axis=dim), axis, backward)
        block = jnp.concatenate([low, block, high], axis=dim)
    return block


def stencil(padded):
    span_x = padded.shape[0] - 8
    span_y = padded.shape[1] - 8
    depth_cells = padded.shape[2]
    deepened = jnp.pad(padded, ((0, 0), (0, 0), (4, 4)))

    def window(shift_x, shift_y, shift_z):
        return deepened[
            4 + shift_x : 4 + shift_x + span_x,
            4 + shift_y : 4 + shift_y + span_y,
            4 + shift_z : 4 + shift_z + depth_cells,
        ]

    summed = 3.0 * STENCIL_COEFFS[0] * window(0, 0, 0)
    for distance in range(1, 5):
        neighbours = window(distance, 0, 0) + window(-distance, 0, 0)
        neighbours = neighbours + window(0, distance, 0) + window(0, -distance, 0)
        neighbours = neighbours + window(0, 0, distance) + window(0, 0, -distance)
        summed = summed + STENCIL_COEFFS[distance] * neighbours
    return summed


def body(
    source_prev,
    source_now,
    receiver_prev,
    receiver_now,
    speed_squared,
    wavelet,
    source_cell,
    traces,
    receiver_cells,
    plan,
    stored_snapshots,
    image_before,
):
    block_x, block_y, depth_cells = source_now.shape
    grid_y = block_y * lax.axis_size("gy")
    start_x = lax.axis_index("gx") * block_x
    start_y = lax.axis_index("gy") * block_y
    total_steps = wavelet.shape[0]
    slot_count = plan.shape[0]
    border = 0
    span_x = block_x + 2 * border
    span_y = block_y + 2 * border
    plane_cells = span_x * span_y
    values = lax.all_gather(traces, ("gx", "gy"), axis=1, tiled=True)
    cell_ids = lax.all_gather(receiver_cells, ("gx", "gy"), axis=1, tiled=True)
    cell_ids = cell_ids[0]
    local_x = cell_ids // grid_y - (start_x - border)
    local_y = cell_ids % grid_y - (start_y - border)
    in_block = (local_x >= 0) & (local_x < span_x) & (local_y >= 0) & (local_y < span_y)
    local_cell = jnp.where(in_block, local_x * span_y + local_y, plane_cells)
    injected = (
        jnp.zeros((total_steps, plane_cells), jnp.float32)
        .at[:, local_cell]
        .add(values, mode="drop")
    )
    injected = injected.reshape(total_steps, span_x, span_y)
    snapshots = jnp.zeros(stored_snapshots.shape, jnp.bfloat16)
    imaged = image_before
    along_x = start_x - 0 + lax.broadcasted_iota(jnp.int32, (block_x + 2 * 0, 1, 1), 0)
    along_y = start_y - 0 + lax.broadcasted_iota(jnp.int32, (1, block_y + 2 * 0, 1), 1)
    along_x, along_y = (along_x, along_y)
    along_z = lax.broadcasted_iota(jnp.int32, (1, 1, depth_cells), 2)
    cell_id = source_cell[0]
    matches = (along_x == cell_id // (grid_y * depth_cells)) & (
        along_y == cell_id // depth_cells % grid_y
    )
    matches = matches & (along_z == cell_id % depth_cells)
    source_core = matches.astype(jnp.float32)
    source_before, source_field = (source_prev, source_now)
    receiver_before, receiver_field = (receiver_prev, receiver_now)
    for step_index in range(total_steps):
        back_time = total_steps - 1 - step_index
        padded = with_halo(jnp.stack([source_field, receiver_field]), (("gx", 1), ("gy", 2)), 4)
        source_spread = stencil(padded[0]) + wavelet[step_index] * source_core
        receiver_spread = stencil(padded[1]).at[:, :, 0].add(injected[back_time])
        source_latest = 2.0 * source_field - source_before + speed_squared * source_spread
        receiver_latest = 2.0 * receiver_field - receiver_before + speed_squared * receiver_spread
        source_before, source_field = (source_field, source_latest)
        receiver_before, receiver_field = (receiver_field, receiver_latest)
        record_matches = plan == step_index
        snapshots = jnp.where(
            record_matches[:, None, None, None], source_field.astype(jnp.bfloat16)[None], snapshots
        )
        correlate_matches = plan == back_time
        slot_index = jnp.sum(
            jnp.where(correlate_matches, jnp.arange(slot_count, dtype=jnp.int32), 0)
        )
        present = jnp.any(correlate_matches)
        snapshot = lax.dynamic_index_in_dim(stored_snapshots, slot_index, 0, keepdims=False).astype(
            jnp.float32
        )
        imaged = imaged + jnp.where(present, snapshot * receiver_field, 0.0)
    source_last, source_final = (source_before, source_field)
    previous, current = (receiver_before, receiver_field)
    return (source_last, source_final, previous, current, snapshots, imaged)


def solution(mesh):
    placed = (
        P(("shot", "gx"), "gy", None),
        P(("shot", "gx"), "gy", None),
        P(("shot", "gx"), "gy", None),
        P(("shot", "gx"), "gy", None),
        P(("shot", "gx"), "gy", None),
        P("shot"),
        P("shot"),
        P("shot", ("gx", "gy")),
        P("shot", ("gx", "gy")),
        P("shot"),
        P("shot", "gx", "gy", None),
        P(("shot", "gx"), "gy", None),
    )
    return jax.shard_map(
        body,
        mesh=mesh,
        in_specs=placed,
        out_specs=(
            P(("shot", "gx"), "gy", None),
            P(("shot", "gx"), "gy", None),
            P(("shot", "gx"), "gy", None),
            P(("shot", "gx"), "gy", None),
            P("shot", "gx", "gy", None),
            P(("shot", "gx"), "gy", None),
        ),
        check_vma=False,
    )
```

profile of v0, /device:TPU:18, one launch (start us, length us, event | category | flops | bytes accessed | tf_op | source)
XLA Modules:
  0.0 254.4 jit_solution(9579591347282151355)
XLA Ops:
  1.6 2.5 collective-permute-start.1
  4.1 3.5 %collective-permute-start = (f32[2,4,8,320]{3,2,1,0:T(8,128)S(1)}, f32[2,4,8,320]{3,2,1,0:T(8,128)S(1)}, u32[]{:S(2)}, u32[]{:S(2)}) collective-permute-start(f32[2,4,8,320]{3,2,1,0:T(8,128)S(1)} %get-tuple-element.250), channel_id=1, source_target_pairs={{0,4},{4,8},{8,12},{1,5},{5,9},{9,13},{2,6},{6,10},{10,14},{3,7},{... | collective-permute-start | bytes 245768 | tf_op jit(solution)/shard_map/ppermute | solution.py:14
  9.7 9.4 %all-reduce.20 = s32[1024]{0:T(1024)S(1)} all-reduce(s32[1024]{0:T(1024)S(1)} %bitcast_dynamic-update-slice_fusion), channel_id=1, replica_groups=mesh['shot'=2,'gx'=4,'gy'=4] {'gx','gy'}, use_global_device_ids=true, to_apply=%add.20 | all-reduce | flops 1024 | bytes 8192
  19.3 1.9 collective-permute-start.3
  21.3 2.4 collective-permute-start.2
  23.8 15.2 %all-gather = f32[16,64,10]{1,2,0:T(8,128)S(1)} all-gather(f32[1,64,10]{1,2,0:T(8,128)S(1)} %bitcast.208), channel_id=1, replica_groups=mesh['shot'=2,'gx'=4,'gy'=4] {'gx','gy'}, dimensions={0}, use_global_device_ids=true | all-gather | bytes 43520 | tf_op jit(solution)/shard_map/all_gather | solution.py:68
  39.2 6.0 %scatter_custom_fusion = f32[10,64]{0,1:T(8,128)S(1)} fusion(s32[1024]{0:T(1024)S(1)} %bitcast.209, f32[1024,10]{1,0:T(8,128)S(1)} %bitcast.206, f32[]{:T(128)} %constant.323.clone.1), kind=kCustom, calls=%fused_computation.926 | custom fusion | flops 10240 | bytes 2564 | tf_op jit(solution)/shard_map/scatter-add | solution.py:78
  49.3 3.3 %collective-permute-start.5 = (f32[2,4,8,320]{3,2,1,0:T(8,128)S(1)}, f32[2,4,8,320]{3,2,1,0:T(8,128)S(1)}, u32[]{:S(2)}, u32[]{:S(2)}) collective-permute-start(f32[2,4,8,320]{3,2,1,0:T(8,128)S(1)} %get-tuple-element.249), channel_id=1, source_target_pairs={{4,0},{8,4},{12,8},{5,1},{9,5},{13,9},{6,2},{10,6},{14,10},{7,3},{... | collective-permute-start | bytes 245768 | tf_op jit(solution)/shard_map/ppermute | solution.py:17
  52.6 2.6 %collective-permute-start.4 = (f32[2,4,8,320]{3,2,1,0:T(8,128)S(1)}, f32[2,4,8,320]{3,2,1,0:T(8,128)S(1)}, u32[]{:S(2)}, u32[]{:S(2)}) collective-permute-start(f32[2,4,8,320]{3,2,1,0:T(8,128)S(1)} %get-tuple-element.248), channel_id=1, source_target_pairs={{0,4},{4,8},{8,12},{1,5},{5,9},{9,13},{2,6},{6,10},{10,14},{3,7},{... | collective-permute-start | bytes 245768 | tf_op jit(solution)/shard_map/ppermute | solution.py:14
  55.2 1.1 collective-permute-done.5
  56.3 4.3 %collective-permute-done.4 = f32[2,4,8,320]{3,2,1,0:T(8,128)S(1)} collective-permute-done((f32[2,4,8,320]{3,2,1,0:T(8,128)S(1)}, f32[2,4,8,320]{3,2,1,0:T(8,128)S(1)}, u32[]{:S(2)}, u32[]{:S(2)}) %collective-permute-start.4) | collective-permute-done | bytes 81952 | tf_op jit(solution)/shard_map/ppermute | solution.py:14
  60.7 3.6 %collective-permute-start.7 = (f32[2,16,4,320]{3,1,2,0:T(8,128)S(1)}, f32[2,16,4,320]{3,1,2,0:T(8,128)S(1)}, u32[]{:S(2)}, u32[]{:S(2)}) collective-permute-start(f32[2,16,4,320]{3,1,2,0:T(8,128)S(1)} %copy.731), channel_id=1, source_target_pairs={{1,0},{2,1},{3,2},{5,4},{6,5},{7,6},{9,8},{10,9},{11,10},{13,12},{... | collective-permute-start | bytes 491528 | tf_op jit(solution)/shard_map/ppermute | solution.py:17
  64.4 1.9 collective-permute-start.6
  66.3 1.2 collective-permute-done.7
  67.6 3.8 %collective-permute-done.6 = f32[2,16,4,320]{3,1,2,0:T(8,128)S(1)} collective-permute-done((f32[2,16,4,320]{3,1,2,0:T(8,128)S(1)}, f32[2,16,4,320]{3,1,2,0:T(8,128)S(1)}, u32[]{:S(2)}, u32[]{:S(2)}) %collective-permute-start.6) | collective-permute-done | bytes 163872 | tf_op jit(solution)/shard_map/ppermute | solution.py:14
  73.1 3.4 %collective-permute-start.9 = (f32[2,4,8,320]{3,2,1,0:T(8,128)S(1)}, f32[2,4,8,320]{3,2,1,0:T(8,128)S(1)}, u32[]{:S(2)}, u32[]{:S(2)}) collective-permute-start(f32[2,4,8,320]{3,2,1,0:T(8,128)S(1)} %get-tuple-element.247), channel_id=1, source_target_pairs={{4,0},{8,4},{12,8},{5,1},{9,5},{13,9},{6,2},{10,6},{14,10},{7,3},{... | collective-permute-start | bytes 245768 | tf_op jit(solution)/shard_map/ppermute | solution.py:17
  76.4 2.5 collective-permute-start.8
  79.6 3.4 %collective-permute-done.8 = f32[2,4,8,320]{3,2,1,0:T(8,128)S(1)} collective-permute-done((f32[2,4,8,320]{3,2,1,0:T(8,128)S(1)}, f32[2,4,8,320]{3,2,1,0:T(8,128)S(1)}, u32[]{:S(2)}, u32[]{:S(2)}) %collective-permute-start.8) | collective-permute-done | bytes 81952 | tf_op jit(solution)/shard_map/ppermute | solution.py:14
  83.1 1.9 collective-permute-start.11
  85.0 2.4 collective-permute-start.10
  88.2 3.8 %collective-permute-done.10 = f32[2,16,4,320]{3,1,2,0:T(8,128)S(1)} collective-permute-done((f32[2,16,4,320]{3,1,2,0:T(8,128)S(1)}, f32[2,16,4,320]{3,1,2,0:T(8,128)S(1)}, u32[]{:S(2)}, u32[]{:S(2)}) %collective-permute-start.10) | collective-permute-done | bytes 163872 | tf_op jit(solution)/shard_map/ppermute | solution.py:14
  93.7 1.9 collective-permute-start.13
  95.7 3.9 %collective-permute-start.12 = (f32[2,4,8,320]{3,2,1,0:T(8,128)S(1)}, f32[2,4,8,320]{3,2,1,0:T(8,128)S(1)}, u32[]{:S(2)}, u32[]{:S(2)}) collective-permute-start(f32[2,4,8,320]{3,2,1,0:T(8,128)S(1)} %get-tuple-element.244), channel_id=1, source_target_pairs={{0,4},{4,8},{8,12},{1,5},{5,9},{9,13},{2,6},{6,10},{10,14},{3,7},{... | collective-permute-start | bytes 245768 | tf_op jit(solution)/shard_map/ppermute | solution.py:14
  100.2 1.9 collective-permute-done.12
  102.3 1.9 collective-permute-start.15
  104.2 2.4 collective-permute-start.14
  107.5 3.8 %collective-permute-done.14 = f32[2,16,4,320]{3,1,2,0:T(8,128)S(1)} collective-permute-done((f32[2,16,4,320]{3,1,2,0:T(8,128)S(1)}, f32[2,16,4,320]{3,1,2,0:T(8,128)S(1)}, u32[]{:S(2)}, u32[]{:S(2)}) %collective-permute-start.14) | collective-permute-done | bytes 163872 | tf_op jit(solution)/shard_map/ppermute | solution.py:14
  113.0 1.9 collective-permute-start.17
  114.9 3.9 %collective-permute-start.16 = (f32[2,4,8,320]{3,2,1,0:T(8,128)S(1)}, f32[2,4,8,320]{3,2,1,0:T(8,128)S(1)}, u32[]{:S(2)}, u32[]{:S(2)}) collective-permute-start(f32[2,4,8,320]{3,2,1,0:T(8,128)S(1)} %get-tuple-element.242), channel_id=1, source_target_pairs={{0,4},{4,8},{8,12},{1,5},{5,9},{9,13},{2,6},{6,10},{10,14},{3,7},{... | collective-permute-start | bytes 245768 | tf_op jit(solution)/shard_map/ppermute | solution.py:14
  119.5 1.9 collective-permute-done.16
  121.5 1.9 collective-permute-start.19
  123.5 2.4 collective-permute-start.18
  126.7 3.8 %collective-permute-done.18 = f32[2,16,4,320]{3,1,2,0:T(8,128)S(1)} collective-permute-done((f32[2,16,4,320]{3,1,2,0:T(8,128)S(1)}, f32[2,16,4,320]{3,1,2,0:T(8,128)S(1)}, u32[]{:S(2)}, u32[]{:S(2)}) %collective-permute-start.18) | collective-permute-done | bytes 163872 | tf_op jit(solution)/shard_map/ppermute | solution.py:14
  132.2 1.9 collective-permute-start.21
  134.2 3.9 %collective-permute-start.20 = (f32[2,4,8,320]{3,2,1,0:T(8,128)S(1)}, f32[2,4,8,320]{3,2,1,0:T(8,128)S(1)}, u32[]{:S(2)}, u32[]{:S(2)}) collective-permute-start(f32[2,4,8,320]{3,2,1,0:T(8,128)S(1)} %get-tuple-element.240), channel_id=1, source_target_pairs={{0,4},{4,8},{8,12},{1,5},{5,9},{9,13},{2,6},{6,10},{10,14},{3,7},{... | collective-permute-start | bytes 245768 | tf_op jit(solution)/shard_map/ppermute | solution.py:14
  138.7 1.9 collective-permute-done.20
  140.8 1.9 collective-permute-start.23
  142.7 2.6 %collective-permute-start.22 = (f32[2,16,4,320]{3,1,2,0:T(8,128)S(1)}, f32[2,16,4,320]{3,1,2,0:T(8,128)S(1)}, u32[]{:S(2)}, u32[]{:S(2)}) collective-permute-start(f32[2,16,4,320]{3,1,2,0:T(8,128)S(1)} %copy.738), channel_id=1, source_target_pairs={{0,1},{1,2},{2,3},{4,5},{5,6},{6,7},{8,9},{9,10},{10,11},{12,13},{... | collective-permute-start | bytes 491528 | tf_op jit(solution)/shard_map/ppermute | solution.py:14
  146.0 3.8 %collective-permute-done.22 = f32[2,16,4,320]{3,1,2,0:T(8,128)S(1)} collective-permute-done((f32[2,16,4,320]{3,1,2,0:T(8,128)S(1)}, f32[2,16,4,320]{3,1,2,0:T(8,128)S(1)}, u32[]{:S(2)}, u32[]{:S(2)}) %collective-permute-start.22) | collective-permute-done | bytes 163872 | tf_op jit(solution)/shard_map/ppermute | solution.py:14
  151.5 1.9 collective-permute-start.25
  153.4 3.9 %collective-permute-start.24 = (f32[2,4,8,320]{3,2,1,0:T(8,128)S(1)}, f32[2,4,8,320]{3,2,1,0:T(8,128)S(1)}, u32[]{:S(2)}, u32[]{:S(2)}) collective-permute-start(f32[2,4,8,320]{3,2,1,0:T(8,128)S(1)} %get-tuple-element.238), channel_id=1, source_target_pairs={{0,4},{4,8},{8,12},{1,5},{5,9},{9,13},{2,6},{6,10},{10,14},{3,7},{... | collective-permute-start | bytes 245768 | tf_op jit(solution)/shard_map/ppermute | solution.py:14
  158.0 1.9 collective-permute-done.24
  160.1 1.9 collective-permute-start.27
  162.0 2.4 collective-permute-start.26
  165.2 3.8 %collective-permute-done.26 = f32[2,16,4,320]{3,1,2,0:T(8,128)S(1)} collective-permute-done((f32[2,16,4,320]{3,1,2,0:T(8,128)S(1)}, f32[2,16,4,320]{3,1,2,0:T(8,128)S(1)}, u32[]{:S(2)}, u32[]{:S(2)}) %collective-permute-start.26) | collective-permute-done | bytes 163872 | tf_op jit(solution)/shard_map/ppermute | solution.py:14
  170.8 1.9 collective-permute-start.29
  172.7 3.9 %collective-permute-start.28 = (f32[2,4,8,320]{3,2,1,0:T(8,128)S(1)}, f32[2,4,8,320]{3,2,1,0:T(8,128)S(1)}, u32[]{:S(2)}, u32[]{:S(2)}) collective-permute-start(f32[2,4,8,320]{3,2,1,0:T(8,128)S(1)} %get-tuple-element.236), channel_id=1, source_target_pairs={{0,4},{4,8},{8,12},{1,5},{5,9},{9,13},{2,6},{6,10},{10,14},{3,7},{... | collective-permute-start | bytes 245768 | tf_op jit(solution)/shard_map/ppermute | solution.py:14
  177.3 1.9 collective-permute-done.28
  179.3 1.9 collective-permute-start.31
  181.3 2.4 collective-permute-start.30
  184.5 3.8 %collective-permute-done.30 = f32[2,16,4,320]{3,1,2,0:T(8,128)S(1)} collective-permute-done((f32[2,16,4,320]{3,1,2,0:T(8,128)S(1)}, f32[2,16,4,320]{3,1,2,0:T(8,128)S(1)}, u32[]{:S(2)}, u32[]{:S(2)}) %collective-permute-start.30) | collective-permute-done | bytes 163872 | tf_op jit(solution)/shard_map/ppermute | solution.py:14
  190.0 1.9 collective-permute-start.33
  191.9 3.9 %collective-permute-start.32 = (f32[2,4,8,320]{3,2,1,0:T(8,128)S(1)}, f32[2,4,8,320]{3,2,1,0:T(8,128)S(1)}, u32[]{:S(2)}, u32[]{:S(2)}) collective-permute-start(f32[2,4,8,320]{3,2,1,0:T(8,128)S(1)} %get-tuple-element.234), channel_id=1, source_target_pairs={{0,4},{4,8},{8,12},{1,5},{5,9},{9,13},{2,6},{6,10},{10,14},{3,7},{... | collective-permute-start | bytes 245768 | tf_op jit(solution)/shard_map/ppermute | solution.py:14
  196.5 1.9 collective-permute-done.32
  198.6 1.9 collective-permute-start.35
  200.5 2.4 collective-permute-start.34
  203.8 3.8 %collective-permute-done.34 = f32[2,16,4,320]{3,1,2,0:T(8,128)S(1)} collective-permute-done((f32[2,16,4,320]{3,1,2,0:T(8,128)S(1)}, f32[2,16,4,320]{3,1,2,0:T(8,128)S(1)}, u32[]{:S(2)}, u32[]{:S(2)}) %collective-permute-start.34) | collective-permute-done | bytes 163872 | tf_op jit(solution)/shard_map/ppermute | solution.py:14
  209.3 2.1 collective-permute-start.37
  211.4 3.9 %collective-permute-start.36 = (f32[2,4,8,320]{3,2,1,0:T(8,128)S(1)}, f32[2,4,8,320]{3,2,1,0:T(8,128)S(1)}, u32[]{:S(2)}, u32[]{:S(2)}) collective-permute-start(f32[2,4,8,320]{3,2,1,0:T(8,128)S(1)} %get-tuple-element.232), channel_id=1, source_target_pairs={{0,4},{4,8},{8,12},{1,5},{5,9},{9,13},{2,6},{6,10},{10,14},{3,7},{... | collective-permute-start | bytes 245768 | tf_op jit(solution)/shard_map/ppermute | solution.py:14
  235.1 1.9 collective-permute-start.39
  237.1 2.4 collective-permute-start.38
  240.4 3.7 %collective-permute-done.38 = f32[2,16,4,320]{3,1,2,0:T(8,128)S(1)} collective-permute-done((f32[2,16,4,320]{3,1,2,0:T(8,128)S(1)}, f32[2,16,4,320]{3,1,2,0:T(8,128)S(1)}, u32[]{:S(2)}, u32[]{:S(2)}) %collective-permute-start.38) | collective-permute-done | bytes 163872 | tf_op jit(solution)/shard_map/ppermute | solution.py:14
  244.8 1.6 fusion.407
  247.3 7.1 %fusion.361 = (f32[8,8,320]{2,1,0:T(8,128)}, f32[8,8,320]{2,1,0:T(8,128)}) fusion(f32[8,8,320]{2,1,0:T(8,128)S(1)} %multiply_add_fusion.1, f32[8,8,320]{2,1,0:T(8,128)S(1)} %multiply_add_fusion.3, f32[8,8,320]{2,1,0:T(8,128)S(1)} %multiply_add_fusion.4, f32[8,8,320]{2,1,0:T(8,128)S(1)} %multiply_add_fusion.8, f32[8,8,320]{2,1,0:T(8,128)S(1)} %copy-done.7, ...), kind=kLoop, calls=%fused_computation.864 | loop fusion | flops 1228800 | bytes 1556530 | tf_op jit(solution)/shard_map/add | solution.py:116
  (199 shorter events, 34.1 us)
Async XLA Ops:
  0.6 7.7 %copy-start.13 = (u32[32]{0:T(128)S(1)}, u32[32]{0:T(128)}, u32[]{:S(2)}) copy-start(u32[32]{0:T(128)} %constant.395) | copy-start | bytes 388
  0.6 8.9 %copy-start.12 = (s32[1,64]{1,0:T(1,128)S(1)}, s32[1,64]{1,0:T(1,128)}, u32[]{:S(2)}) copy-start(s32[1,64]{1,0:T(1,128)} %param.40) | copy-start | bytes 772
  0.7 18.6 %copy-start.4 = (f32[8,8,320]{2,1,0:T(8,128)S(1)}, f32[8,8,320]{2,1,0:T(8,128)}, u32[]{:S(2)}) copy-start(f32[8,8,320]{2,1,0:T(8,128)} %param.35) | copy-start | bytes 245764
  1.6 17.6 %copy-start.1 = (f32[8,8,320]{2,1,0:T(8,128)S(1)}, f32[8,8,320]{2,1,0:T(8,128)}, u32[]{:S(2)}) copy-start(f32[8,8,320]{2,1,0:T(8,128)} %param.33) | copy-start | bytes 245764
  1.6 17.6 %collective-permute-start.1 = (f32[2,4,8,320]{3,2,1,0:T(8,128)S(1)}, f32[2,4,8,320]{3,2,1,0:T(8,128)S(1)}, u32[]{:S(2)}, u32[]{:S(2)}) collective-permute-start(f32[2,4,8,320]{3,2,1,0:T(8,128)S(1)} %get-tuple-element.251), channel_id=1, source_target_pairs={{4,0},{8,4},{12,8},{5,1},{9,5},{13,9},{6,2},{10,6},{14,10},{7,3},{... | collective-permute-start | bytes 245768 | tf_op jit(solution)/shard_map/ppermute | solution.py:17
  4.1 15.1 %collective-permute-start = (f32[2,4,8,320]{3,2,1,0:T(8,128)S(1)}, f32[2,4,8,320]{3,2,1,0:T(8,128)S(1)}, u32[]{:S(2)}, u32[]{:S(2)}) collective-permute-start(f32[2,4,8,320]{3,2,1,0:T(8,128)S(1)} %get-tuple-element.250), channel_id=1, source_target_pairs={{0,4},{4,8},{8,12},{1,5},{5,9},{9,13},{2,6},{6,10},{10,14},{3,7},{... | collective-permute-start | bytes 245768 | tf_op jit(solution)/shard_map/ppermute | solution.py:14
  19.3 26.6 %collective-permute-start.3 = (f32[2,16,4,320]{3,1,2,0:T(8,128)S(1)}, f32[2,16,4,320]{3,1,2,0:T(8,128)S(1)}, u32[]{:S(2)}, u32[]{:S(2)}) collective-permute-start(f32[2,16,4,320]{3,1,2,0:T(8,128)S(1)} %copy.729), channel_id=1, source_target_pairs={{1,0},{2,1},{3,2},{5,4},{6,5},{7,6},{9,8},{10,9},{11,10},{13,12},{... | collective-permute-start | bytes 491528 | tf_op jit(solution)/shard_map/ppermute | solution.py:17
  21.3 2.5 copy-start.10
  21.3 24.7 %collective-permute-start.2 = (f32[2,16,4,320]{3,1,2,0:T(8,128)S(1)}, f32[2,16,4,320]{3,1,2,0:T(8,128)S(1)}, u32[]{:S(2)}, u32[]{:S(2)}) collective-permute-start(f32[2,16,4,320]{3,1,2,0:T(8,128)S(1)} %copy.728), channel_id=1, source_target_pairs={{0,1},{1,2},{2,3},{4,5},{5,6},{6,7},{8,9},{9,10},{10,11},{12,13},{... | collective-permute-start | bytes 491528 | tf_op jit(solution)/shard_map/ppermute | solution.py:14
  39.0 6.3 %copy-start.9 = (f32[10]{0:T(128)S(1)}, f32[10]{0:T(128)}, u32[]{:S(2)}) copy-start(f32[10]{0:T(128)} %param.37) | copy-start | bytes 124
  46.4 0.9 copy-start.8
  46.7 0.9 copy-start
  47.6 0.9 copy-start.6
  49.3 6.9 %collective-permute-start.5 = (f32[2,4,8,320]{3,2,1,0:T(8,128)S(1)}, f32[2,4,8,320]{3,2,1,0:T(8,128)S(1)}, u32[]{:S(2)}, u32[]{:S(2)}) collective-permute-start(f32[2,4,8,320]{3,2,1,0:T(8,128)S(1)} %get-tuple-element.249), channel_id=1, source_target_pairs={{4,0},{8,4},{12,8},{5,1},{9,5},{13,9},{6,2},{10,6},{14,10},{7,3},{... | collective-permute-start | bytes 245768 | tf_op jit(solution)/shard_map/ppermute | solution.py:17
  52.6 8.0 %collective-permute-start.4 = (f32[2,4,8,320]{3,2,1,0:T(8,128)S(1)}, f32[2,4,8,320]{3,2,1,0:T(8,128)S(1)}, u32[]{:S(2)}, u32[]{:S(2)}) collective-permute-start(f32[2,4,8,320]{3,2,1,0:T(8,128)S(1)} %get-tuple-element.248), channel_id=1, source_target_pairs={{0,4},{4,8},{8,12},{1,5},{5,9},{9,13},{2,6},{6,10},{10,14},{3,7},{... | collective-permute-start | bytes 245768 | tf_op jit(solution)/shard_map/ppermute | solution.py:14
  60.7 6.8 %collective-permute-start.7 = (f32[2,16,4,320]{3,1,2,0:T(8,128)S(1)}, f32[2,16,4,320]{3,1,2,0:T(8,128)S(1)}, u32[]{:S(2)}, u32[]{:S(2)}) collective-permute-start(f32[2,16,4,320]{3,1,2,0:T(8,128)S(1)} %copy.731), channel_id=1, source_target_pairs={{1,0},{2,1},{3,2},{5,4},{6,5},{7,6},{9,8},{10,9},{11,10},{13,12},{... | collective-permute-start | bytes 491528 | tf_op jit(solution)/shard_map/ppermute | solution.py:17
  64.4 7.0 %collective-permute-start.6 = (f32[2,16,4,320]{3,1,2,0:T(8,128)S(1)}, f32[2,16,4,320]{3,1,2,0:T(8,128)S(1)}, u32[]{:S(2)}, u32[]{:S(2)}) collective-permute-start(f32[2,16,4,320]{3,1,2,0:T(8,128)S(1)} %copy.730), channel_id=1, source_target_pairs={{0,1},{1,2},{2,3},{4,5},{5,6},{6,7},{8,9},{9,10},{10,11},{12,13},{... | collective-permute-start | bytes 491528 | tf_op jit(solution)/shard_map/ppermute | solution.py:14
  73.1 6.5 %collective-permute-start.9 = (f32[2,4,8,320]{3,2,1,0:T(8,128)S(1)}, f32[2,4,8,320]{3,2,1,0:T(8,128)S(1)}, u32[]{:S(2)}, u32[]{:S(2)}) collective-permute-start(f32[2,4,8,320]{3,2,1,0:T(8,128)S(1)} %get-tuple-element.247), channel_id=1, source_target_pairs={{4,0},{8,4},{12,8},{5,1},{9,5},{13,9},{6,2},{10,6},{14,10},{7,3},{... | collective-permute-start | bytes 245768 | tf_op jit(solution)/shard_map/ppermute | solution.py:17
  76.4 6.5 %collective-permute-start.8 = (f32[2,4,8,320]{3,2,1,0:T(8,128)S(1)}, f32[2,4,8,320]{3,2,1,0:T(8,128)S(1)}, u32[]{:S(2)}, u32[]{:S(2)}) collective-permute-start(f32[2,4,8,320]{3,2,1,0:T(8,128)S(1)} %get-tuple-element.246), channel_id=1, source_target_pairs={{0,4},{4,8},{8,12},{1,5},{5,9},{9,13},{2,6},{6,10},{10,14},{3,7},{... | collective-permute-start | bytes 245768 | tf_op jit(solution)/shard_map/ppermute | solution.py:14
  83.1 5.1 %collective-permute-start.11 = (f32[2,16,4,320]{3,1,2,0:T(8,128)S(1)}, f32[2,16,4,320]{3,1,2,0:T(8,128)S(1)}, u32[]{:S(2)}, u32[]{:S(2)}) collective-permute-start(f32[2,16,4,320]{3,1,2,0:T(8,128)S(1)} %copy.733), channel_id=1, source_target_pairs={{1,0},{2,1},{3,2},{5,4},{6,5},{7,6},{9,8},{10,9},{11,10},{13,12},{... | collective-permute-start | bytes 491528 | tf_op jit(solution)/shard_map/ppermute | solution.py:17
  85.0 7.0 %collective-permute-start.10 = (f32[2,16,4,320]{3,1,2,0:T(8,128)S(1)}, f32[2,16,4,320]{3,1,2,0:T(8,128)S(1)}, u32[]{:S(2)}, u32[]{:S(2)}) collective-permute-start(f32[2,16,4,320]{3,1,2,0:T(8,128)S(1)} %copy.732), channel_id=1, source_target_pairs={{0,1},{1,2},{2,3},{4,5},{5,6},{6,7},{8,9},{9,10},{10,11},{12,13},{... | collective-permute-start | bytes 491528 | tf_op jit(solution)/shard_map/ppermute | solution.py:14
  93.7 6.5 %collective-permute-start.13 = (f32[2,4,8,320]{3,2,1,0:T(8,128)S(1)}, f32[2,4,8,320]{3,2,1,0:T(8,128)S(1)}, u32[]{:S(2)}, u32[]{:S(2)}) collective-permute-start(f32[2,4,8,320]{3,2,1,0:T(8,128)S(1)} %get-tuple-element.245), channel_id=1, source_target_pairs={{4,0},{8,4},{12,8},{5,1},{9,5},{13,9},{6,2},{10,6},{14,10},{7,3},{... | collective-permute-start | bytes 245768 | tf_op jit(solution)/shard_map/ppermute | solution.py:17
  95.7 6.5 %collective-permute-start.12 = (f32[2,4,8,320]{3,2,1,0:T(8,128)S(1)}, f32[2,4,8,320]{3,2,1,0:T(8,128)S(1)}, u32[]{:S(2)}, u32[]{:S(2)}) collective-permute-start(f32[2,4,8,320]{3,2,1,0:T(8,128)S(1)} %get-tuple-element.244), channel_id=1, source_target_pairs={{0,4},{4,8},{8,12},{1,5},{5,9},{9,13},{2,6},{6,10},{10,14},{3,7},{... | collective-permute-start | bytes 245768 | tf_op jit(solution)/shard_map/ppermute | solution.py:14
  102.3 5.1 %collective-permute-start.15 = (f32[2,16,4,320]{3,1,2,0:T(8,128)S(1)}, f32[2,16,4,320]{3,1,2,0:T(8,128)S(1)}, u32[]{:S(2)}, u32[]{:S(2)}) collective-permute-start(f32[2,16,4,320]{3,1,2,0:T(8,128)S(1)} %copy.735), channel_id=1, source_target_pairs={{1,0},{2,1},{3,2},{5,4},{6,5},{7,6},{9,8},{10,9},{11,10},{13,12},{... | collective-permute-start | bytes 491528 | tf_op jit(solution)/shard_map/ppermute | solution.py:17
  104.2 7.0 %collective-permute-start.14 = (f32[2,16,4,320]{3,1,2,0:T(8,128)S(1)}, f32[2,16,4,320]{3,1,2,0:T(8,128)S(1)}, u32[]{:S(2)}, u32[]{:S(2)}) collective-permute-start(f32[2,16,4,320]{3,1,2,0:T(8,128)S(1)} %copy.734), channel_id=1, source_target_pairs={{0,1},{1,2},{2,3},{4,5},{5,6},{6,7},{8,9},{9,10},{10,11},{12,13},{... | collective-permute-start | bytes 491528 | tf_op jit(solution)/shard_map/ppermute | solution.py:14
  113.0 6.5 %collective-permute-start.17 = (f32[2,4,8,320]{3,2,1,0:T(8,128)S(1)}, f32[2,4,8,320]{3,2,1,0:T(8,128)S(1)}, u32[]{:S(2)}, u32[]{:S(2)}) collective-permute-start(f32[2,4,8,320]{3,2,1,0:T(8,128)S(1)} %get-tuple-element.243), channel_id=1, source_target_pairs={{4,0},{8,4},{12,8},{5,1},{9,5},{13,9},{6,2},{10,6},{14,10},{7,3},{... | collective-permute-start | bytes 245768 | tf_op jit(solution)/shard_map/ppermute | solution.py:17
  114.9 6.5 %collective-permute-start.16 = (f32[2,4,8,320]{3,2,1,0:T(8,128)S(1)}, f32[2,4,8,320]{3,2,1,0:T(8,128)S(1)}, u32[]{:S(2)}, u32[]{:S(2)}) collective-permute-start(f32[2,4,8,320]{3,2,1,0:T(8,128)S(1)} %get-tuple-element.242), channel_id=1, source_target_pairs={{0,4},{4,8},{8,12},{1,5},{5,9},{9,13},{2,6},{6,10},{10,14},{3,7},{... | collective-permute-start | bytes 245768 | tf_op jit(solution)/shard_map/ppermute | solution.py:14
  121.5 5.1 %collective-permute-start.19 = (f32[2,16,4,320]{3,1,2,0:T(8,128)S(1)}, f32[2,16,4,320]{3,1,2,0:T(8,128)S(1)}, u32[]{:S(2)}, u32[]{:S(2)}) collective-permute-start(f32[2,16,4,320]{3,1,2,0:T(8,128)S(1)} %copy.737), channel_id=1, source_target_pairs={{1,0},{2,1},{3,2},{5,4},{6,5},{7,6},{9,8},{10,9},{11,10},{13,12},{... | collective-permute-start | bytes 491528 | tf_op jit(solution)/shard_map/ppermute | solution.py:17
  123.5 7.0 %collective-permute-start.18 = (f32[2,16,4,320]{3,1,2,0:T(8,128)S(1)}, f32[2,16,4,320]{3,1,2,0:T(8,128)S(1)}, u32[]{:S(2)}, u32[]{:S(2)}) collective-permute-start(f32[2,16,4,320]{3,1,2,0:T(8,128)S(1)} %copy.736), channel_id=1, source_target_pairs={{0,1},{1,2},{2,3},{4,5},{5,6},{6,7},{8,9},{9,10},{10,11},{12,13},{... | collective-permute-start | bytes 491528 | tf_op jit(solution)/shard_map/ppermute | solution.py:14
  132.2 6.5 %collective-permute-start.21 = (f32[2,4,8,320]{3,2,1,0:T(8,128)S(1)}, f32[2,4,8,320]{3,2,1,0:T(8,128)S(1)}, u32[]{:S(2)}, u32[]{:S(2)}) collective-permute-start(f32[2,4,8,320]{3,2,1,0:T(8,128)S(1)} %get-tuple-element.241), channel_id=1, source_target_pairs={{4,0},{8,4},{12,8},{5,1},{9,5},{13,9},{6,2},{10,6},{14,10},{7,3},{... | collective-permute-start | bytes 245768 | tf_op jit(solution)/shard_map/ppermute | solution.py:17
  134.2 6.5 %collective-permute-start.20 = (f32[2,4,8,320]{3,2,1,0:T(8,128)S(1)}, f32[2,4,8,320]{3,2,1,0:T(8,128)S(1)}, u32[]{:S(2)}, u32[]{:S(2)}) collective-permute-start(f32[2,4,8,320]{3,2,1,0:T(8,128)S(1)} %get-tuple-element.240), channel_id=1, source_target_pairs={{0,4},{4,8},{8,12},{1,5},{5,9},{9,13},{2,6},{6,10},{10,14},{3,7},{... | collective-permute-start | bytes 245768 | tf_op jit(solution)/shard_map/ppermute | solution.py:14
  140.8 5.1 %collective-permute-start.23 = (f32[2,16,4,320]{3,1,2,0:T(8,128)S(1)}, f32[2,16,4,320]{3,1,2,0:T(8,128)S(1)}, u32[]{:S(2)}, u32[]{:S(2)}) collective-permute-start(f32[2,16,4,320]{3,1,2,0:T(8,128)S(1)} %copy.739), channel_id=1, source_target_pairs={{1,0},{2,1},{3,2},{5,4},{6,5},{7,6},{9,8},{10,9},{11,10},{13,12},{... | collective-permute-start | bytes 491528 | tf_op jit(solution)/shard_map/ppermute | solution.py:17
  142.7 7.0 %collective-permute-start.22 = (f32[2,16,4,320]{3,1,2,0:T(8,128)S(1)}, f32[2,16,4,320]{3,1,2,0:T(8,128)S(1)}, u32[]{:S(2)}, u32[]{:S(2)}) collective-permute-start(f32[2,16,4,320]{3,1,2,0:T(8,128)S(1)} %copy.738), channel_id=1, source_target_pairs={{0,1},{1,2},{2,3},{4,5},{5,6},{6,7},{8,9},{9,10},{10,11},{12,13},{... | collective-permute-start | bytes 491528 | tf_op jit(solution)/shard_map/ppermute | solution.py:14
  151.5 6.5 %collective-permute-start.25 = (f32[2,4,8,320]{3,2,1,0:T(8,128)S(1)}, f32[2,4,8,320]{3,2,1,0:T(8,128)S(1)}, u32[]{:S(2)}, u32[]{:S(2)}) collective-permute-start(f32[2,4,8,320]{3,2,1,0:T(8,128)S(1)} %get-tuple-element.239), channel_id=1, source_target_pairs={{4,0},{8,4},{12,8},{5,1},{9,5},{13,9},{6,2},{10,6},{14,10},{7,3},{... | collective-permute-start | bytes 245768 | tf_op jit(solution)/shard_map/ppermute | solution.py:17
  153.4 6.5 %collective-permute-start.24 = (f32[2,4,8,320]{3,2,1,0:T(8,128)S(1)}, f32[2,4,8,320]{3,2,1,0:T(8,128)S(1)}, u32[]{:S(2)}, u32[]{:S(2)}) collective-permute-start(f32[2,4,8,320]{3,2,1,0:T(8,128)S(1)} %get-tuple-element.238), channel_id=1, source_target_pairs={{0,4},{4,8},{8,12},{1,5},{5,9},{9,13},{2,6},{6,10},{10,14},{3,7},{... | collective-permute-start | bytes 245768 | tf_op jit(solution)/shard_map/ppermute | solution.py:14
  160.1 5.1 %collective-permute-start.27 = (f32[2,16,4,320]{3,1,2,0:T(8,128)S(1)}, f32[2,16,4,320]{3,1,2,0:T(8,128)S(1)}, u32[]{:S(2)}, u32[]{:S(2)}) collective-permute-start(f32[2,16,4,320]{3,1,2,0:T(8,128)S(1)} %copy.741), channel_id=1, source_target_pairs={{1,0},{2,1},{3,2},{5,4},{6,5},{7,6},{9,8},{10,9},{11,10},{13,12},{... | collective-permute-start | bytes 491528 | tf_op jit(solution)/shard_map/ppermute | solution.py:17
  162.0 7.0 %collective-permute-start.26 = (f32[2,16,4,320]{3,1,2,0:T(8,128)S(1)}, f32[2,16,4,320]{3,1,2,0:T(8,128)S(1)}, u32[]{:S(2)}, u32[]{:S(2)}) collective-permute-start(f32[2,16,4,320]{3,1,2,0:T(8,128)S(1)} %copy.740), channel_id=1, source_target_pairs={{0,1},{1,2},{2,3},{4,5},{5,6},{6,7},{8,9},{9,10},{10,11},{12,13},{... | collective-permute-start | bytes 491528 | tf_op jit(solution)/shard_map/ppermute | solution.py:14
  170.8 6.5 %collective-permute-start.29 = (f32[2,4,8,320]{3,2,1,0:T(8,128)S(1)}, f32[2,4,8,320]{3,2,1,0:T(8,128)S(1)}, u32[]{:S(2)}, u32[]{:S(2)}) collective-permute-start(f32[2,4,8,320]{3,2,1,0:T(8,128)S(1)} %get-tuple-element.237), channel_id=1, source_target_pairs={{4,0},{8,4},{12,8},{5,1},{9,5},{13,9},{6,2},{10,6},{14,10},{7,3},{... | collective-permute-start | bytes 245768 | tf_op jit(solution)/shard_map/ppermute | solution.py:17
  172.7 6.5 %collective-permute-start.28 = (f32[2,4,8,320]{3,2,1,0:T(8,128)S(1)}, f32[2,4,8,320]{3,2,1,0:T(8,128)S(1)}, u32[]{:S(2)}, u32[]{:S(2)}) collective-permute-start(f32[2,4,8,320]{3,2,1,0:T(8,128)S(1)} %get-tuple-element.236), channel_id=1, source_target_pairs={{0,4},{4,8},{8,12},{1,5},{5,9},{9,13},{2,6},{6,10},{10,14},{3,7},{... | collective-permute-start | bytes 245768 | tf_op jit(solution)/shard_map/ppermute | solution.py:14
  179.3 5.1 %collective-permute-start.31 = (f32[2,16,4,320]{3,1,2,0:T(8,128)S(1)}, f32[2,16,4,320]{3,1,2,0:T(8,128)S(1)}, u32[]{:S(2)}, u32[]{:S(2)}) collective-permute-start(f32[2,16,4,320]{3,1,2,0:T(8,128)S(1)} %copy.743), channel_id=1, source_target_pairs={{1,0},{2,1},{3,2},{5,4},{6,5},{7,6},{9,8},{10,9},{11,10},{13,12},{... | collective-permute-start | bytes 491528 | tf_op jit(solution)/shard_map/ppermute | solution.py:17
  181.3 7.0 %collective-permute-start.30 = (f32[2,16,4,320]{3,1,2,0:T(8,128)S(1)}, f32[2,16,4,320]{3,1,2,0:T(8,128)S(1)}, u32[]{:S(2)}, u32[]{:S(2)}) collective-permute-start(f32[2,16,4,320]{3,1,2,0:T(8,128)S(1)} %copy.742), channel_id=1, source_target_pairs={{0,1},{1,2},{2,3},{4,5},{5,6},{6,7},{8,9},{9,10},{10,11},{12,13},{... | collective-permute-start | bytes 491528 | tf_op jit(solution)/shard_map/ppermute | solution.py:14
  190.0 6.5 %collective-permute-start.33 = (f32[2,4,8,320]{3,2,1,0:T(8,128)S(1)}, f32[2,4,8,320]{3,2,1,0:T(8,128)S(1)}, u32[]{:S(2)}, u32[]{:S(2)}) collective-permute-start(f32[2,4,8,320]{3,2,1,0:T(8,128)S(1)} %get-tuple-element.235), channel_id=1, source_target_pairs={{4,0},{8,4},{12,8},{5,1},{9,5},{13,9},{6,2},{10,6},{14,10},{7,3},{... | collective-permute-start | bytes 245768 | tf_op jit(solution)/shard_map/ppermute | solution.py:17
  191.9 6.5 %collective-permute-start.32 = (f32[2,4,8,320]{3,2,1,0:T(8,128)S(1)}, f32[2,4,8,320]{3,2,1,0:T(8,128)S(1)}, u32[]{:S(2)}, u32[]{:S(2)}) collective-permute-start(f32[2,4,8,320]{3,2,1,0:T(8,128)S(1)} %get-tuple-element.234), channel_id=1, source_target_pairs={{0,4},{4,8},{8,12},{1,5},{5,9},{9,13},{2,6},{6,10},{10,14},{3,7},{... | collective-permute-start | bytes 245768 | tf_op jit(solution)/shard_map/ppermute | solution.py:14
  198.6 5.1 %collective-permute-start.35 = (f32[2,16,4,320]{3,1,2,0:T(8,128)S(1)}, f32[2,16,4,320]{3,1,2,0:T(8,128)S(1)}, u32[]{:S(2)}, u32[]{:S(2)}) collective-permute-start(f32[2,16,4,320]{3,1,2,0:T(8,128)S(1)} %copy.745), channel_id=1, source_target_pairs={{1,0},{2,1},{3,2},{5,4},{6,5},{7,6},{9,8},{10,9},{11,10},{13,12},{... | collective-permute-start | bytes 491528 | tf_op jit(solution)/shard_map/ppermute | solution.py:17
  200.5 7.0 %collective-permute-start.34 = (f32[2,16,4,320]{3,1,2,0:T(8,128)S(1)}, f32[2,16,4,320]{3,1,2,0:T(8,128)S(1)}, u32[]{:S(2)}, u32[]{:S(2)}) collective-permute-start(f32[2,16,4,320]{3,1,2,0:T(8,128)S(1)} %copy.744), channel_id=1, source_target_pairs={{0,1},{1,2},{2,3},{4,5},{5,6},{6,7},{8,9},{9,10},{10,11},{12,13},{... | collective-permute-start | bytes 491528 | tf_op jit(solution)/shard_map/ppermute | solution.py:14
  208.3 38.9 %copy-start.3 = (f32[8,8,320]{2,1,0:T(8,128)}, f32[8,8,320]{2,1,0:T(8,128)S(1)}, u32[]{:S(2)}) copy-start(f32[8,8,320]{2,1,0:T(8,128)S(1)} %multiply_add_fusion.1) | copy-start | bytes 245764
  209.3 35.5 %copy-start.2 = (f32[8,8,320]{2,1,0:T(8,128)}, f32[8,8,320]{2,1,0:T(8,128)S(1)}, u32[]{:S(2)}) copy-start(f32[8,8,320]{2,1,0:T(8,128)S(1)} %get-tuple-element.175) | copy-start | bytes 245764
  209.3 6.0 %copy-start.11 = (s32[4]{0:T(128)S(1)}, s32[4]{0:T(128)}, u32[]{:S(2)}) copy-start(s32[4]{0:T(128)} %param.41) | copy-start | bytes 52
  209.3 25.6 %collective-permute-start.37 = (f32[2,4,8,320]{3,2,1,0:T(8,128)S(1)}, f32[2,4,8,320]{3,2,1,0:T(8,128)S(1)}, u32[]{:S(2)}, u32[]{:S(2)}) collective-permute-start(f32[2,4,8,320]{3,2,1,0:T(8,128)S(1)} %get-tuple-element.233), channel_id=1, source_target_pairs={{4,0},{8,4},{12,8},{5,1},{9,5},{13,9},{6,2},{10,6},{14,10},{7,3},{... | collective-permute-start | bytes 245768 | tf_op jit(solution)/shard_map/ppermute | solution.py:17
  211.4 23.6 %collective-permute-start.36 = (f32[2,4,8,320]{3,2,1,0:T(8,128)S(1)}, f32[2,4,8,320]{3,2,1,0:T(8,128)S(1)}, u32[]{:S(2)}, u32[]{:S(2)}) collective-permute-start(f32[2,4,8,320]{3,2,1,0:T(8,128)S(1)} %get-tuple-element.232), channel_id=1, source_target_pairs={{0,4},{4,8},{8,12},{1,5},{5,9},{9,13},{2,6},{6,10},{10,14},{3,7},{... | collective-permute-start | bytes 245768 | tf_op jit(solution)/shard_map/ppermute | solution.py:14
  235.1 5.2 %collective-permute-start.39 = (f32[2,16,4,320]{3,1,2,0:T(8,128)S(1)}, f32[2,16,4,320]{3,1,2,0:T(8,128)S(1)}, u32[]{:S(2)}, u32[]{:S(2)}) collective-permute-start(f32[2,16,4,320]{3,1,2,0:T(8,128)S(1)} %copy.747), channel_id=1, source_target_pairs={{1,0},{2,1},{3,2},{5,4},{6,5},{7,6},{9,8},{10,9},{11,10},{13,12},{... | collective-permute-start | bytes 491528 | tf_op jit(solution)/shard_map/ppermute | solution.py:17
  237.1 7.0 %collective-permute-start.38 = (f32[2,16,4,320]{3,1,2,0:T(8,128)S(1)}, f32[2,16,4,320]{3,1,2,0:T(8,128)S(1)}, u32[]{:S(2)}, u32[]{:S(2)}) collective-permute-start(f32[2,16,4,320]{3,1,2,0:T(8,128)S(1)} %copy.746), channel_id=1, source_target_pairs={{0,1},{1,2},{2,3},{4,5},{5,6},{6,7},{8,9},{9,10},{10,11},{12,13},{... | collective-permute-start | bytes 491528 | tf_op jit(solution)/shard_map/ppermute | solution.py:14
  246.3 0.9 copy-start.5
  246.3 1.0 copy-start.7
where the time goes:
time: 256 us; the launch traced here: 254 us
  starting transfers between devices  103 us (40%)
  waiting for transfers between devices  64.8 us (25%)
  other arithmetic  32.2 us (13%)
  blocking collectives  24.6 us (10%)
  between operations  22.2 us (9%)
  local copies, waits for them, and re-layouts  7.13 us (3%)
    ppermute x20, starting transfers between devices, with_halo(): lax.ppermute(lax.slice_in_dim(block, block.shape[dim] - width, None, axis...  59.8 us
    ppermute x20, waiting for transfers between devices, with_halo(): lax.ppermute(lax.slice_in_dim(block, block.shape[dim] - width, None, axis...  53 us
    ppermute x20, starting transfers between devices, with_halo(): lax.ppermute(lax.slice_in_dim(block, 0, width, axis=dim), axis, backward)  43.6 us
    all_gather x1, blocking collectives, body(): values = lax.all_gather(traces, ('gx', 'gy'), axis=1, tiled=True)  15.2 us
    ppermute x20, waiting for transfers between devices, with_halo(): lax.ppermute(lax.slice_in_dim(block, 0, width, axis=dim), axis, backward)  11.7 us
    convert_element_type x10, other arithmetic, body(): source_field.astype(jnp.bfloat16)[None]  9.89 us
    unnamed x1, blocking collectives  9.37 us
    add x1, other arithmetic, body(): imaged = imaged + jnp.where(present, snapshot * receiver_field, 0.0)  7.05 us
  transfers between devices with their start and end apart: 40, of which 33 were waited for; matrix products, arithmetic and copies ran while one was open for 4% of the time, Pallas kernels for 0%

commit v1 on v0

--- a/solution.py
+++ b/solution.py
@@ -65,7 +65,15 @@
     span_x = block_x + 2 * border
     span_y = block_y + 2 * border
     plane_cells = span_x * span_y
-    values = lax.all_gather(traces, ("gx", "gy"), axis=1, tiled=True)
+    ways, here, step = (lax.axis_size(("gx", "gy")), lax.axis_index(("gx", "gy")), traces.shape[1])
+    line, have = (traces, 1)
+    while have < ways:
+        line = jnp.concatenate(
+            [line, lax.ppermute(line, ("gx", "gy"), [(d, (d - have) % ways) for d in range(ways)])],
+            axis=1,
+        )
+        have = 2 * have
+    values = jnp.roll(line, here * step, axis=1)
     cell_ids = lax.all_gather(receiver_cells, ("gx", "gy"), axis=1, tiled=True)
     cell_ids = cell_ids[0]
     local_x = cell_ids // grid_y - (start_x - border)

time: 256 us -> 250 us (0.977)
  blocking collectives: 24.6 us -> 9.37 us
  starting transfers between devices: 103 us -> 108 us
  waiting for transfers between devices: 64.8 us -> 68.4 us
    all_gather x1 -> x0, blocking collectives: 15.2 us -> none  [body(): values = lax.all_gather(traces, ('gx', 'gy'), axis=1, tiled=True)]
    ppermute x0 -> x4, waiting for transfers between devices: none -> 6.28 us  [body(): lax.ppermute(line, ('gx', 'gy'), [(d, (d - have) % ways) for d in range(w...]
    ppermute x0 -> x4, starting transfers between devices: none -> 4.79 us  [body(): lax.ppermute(line, ('gx', 'gy'), [(d, (d - have) % ways) for d in range(w...]
  transfers between devices with their start and end apart: 40 -> 44, of which waited for: 33 -> 35; matrix products, arithmetic and copies ran while one was open for 4% -> 4% of each run, Pallas kernels for 0% -> 0%
where the time goes in v1:
time: 250 us; the launch traced here: 248 us
  starting transfers between devices  108 us (43%)
  waiting for transfers between devices  68.4 us (27%)
  other arithmetic  32.4 us (13%)
  between operations  22.2 us (9%)
  blocking collectives  9.37 us (4%)
  local copies, waits for them, and re-layouts  7.91 us (3%)
    ppermute x20, starting transfers between devices, with_halo(): lax.ppermute(lax.slice_in_dim(block, block.shape[dim] - width, None, axis...  61 us
    ppermute x20, waiting for transfers between devices, with_halo(): lax.ppermute(lax.slice_in_dim(block, block.shape[dim] - width, None, axis...  51.7 us
    ppermute x20, starting transfers between devices, with_halo(): lax.ppermute(lax.slice_in_dim(block, 0, width, axis=dim), axis, backward)  42.2 us
    ppermute x20, waiting for transfers between devices, with_halo(): lax.ppermute(lax.slice_in_dim(block, 0, width, axis=dim), axis, backward)  10.4 us
    convert_element_type x10, other arithmetic, body(): source_field.astype(jnp.bfloat16)[None]  9.9 us
    unnamed x1, blocking collectives  9.37 us
    add x1, other arithmetic, body(): imaged = imaged + jnp.where(present, snapshot * receiver_field, 0.0)  7.04 us
    ppermute x4, waiting for transfers between devices, body(): lax.ppermute(line, ('gx', 'gy'), [(d, (d - have) % ways) for d in range(w...  6.28 us
  transfers between devices with their start and end apart: 44, of which 35 were waited for; matrix products, arithmetic and copies ran while one was open for 4% of the time, Pallas kernels for 0%

profile of v1, /device:TPU:18, one launch (start us, length us, event | category | flops | bytes accessed | tf_op | source)
XLA Modules:
  0.0 248.4 jit_solution(18370803998945440927)
XLA Ops:
  1.5 2.4 collective-permute-start.1
  3.9 3.5 %collective-permute-start = (f32[2,4,8,320]{3,2,1,0:T(8,128)S(1)}, f32[2,4,8,320]{3,2,1,0:T(8,128)S(1)}, u32[]{:S(2)}, u32[]{:S(2)}) collective-permute-start(f32[2,4,8,320]{3,2,1,0:T(8,128)S(1)} %get-tuple-element.250), channel_id=1, source_target_pairs={{0,4},{4,8},{8,12},{1,5},{5,9},{9,13},{2,6},{6,10},{10,14},{3,7},{... | collective-permute-start | bytes 245768 | tf_op jit(solution)/shard_map/ppermute | solution.py:14
  10.2 9.4 %all-reduce.20 = s32[1024]{0:T(1024)S(1)} all-reduce(s32[1024]{0:T(1024)S(1)} %bitcast_dynamic-update-slice_fusion), channel_id=1, replica_groups=mesh['shot'=2,'gx'=4,'gy'=4] {'gx','gy'}, use_global_device_ids=true, to_apply=%add.20 | all-reduce | flops 1024 | bytes 8192
  21.0 3.3 %collective-permute-done.5 = f32[10,128]{1,0:T(8,128)S(1)} collective-permute-done((f32[10,128]{1,0:T(8,128)S(1)}, f32[10,128]{1,0:T(8,128)S(1)}, u32[]{:S(2)}, u32[]{:S(2)}) %collective-permute-start.5) | collective-permute-done | bytes 5152 | tf_op jit(solution)/shard_map/ppermute | solution.py:72
  26.7 3.0 %collective-permute-done.6 = f32[10,256]{1,0:T(8,128)S(1)} collective-permute-done((f32[10,256]{1,0:T(8,128)S(1)}, f32[10,256]{1,0:T(8,128)S(1)}, u32[]{:S(2)}, u32[]{:S(2)}) %collective-permute-start.6) | collective-permute-done | bytes 10272 | tf_op jit(solution)/shard_map/ppermute | solution.py:72
  29.7 2.0 collective-permute-start.7
  31.8 1.9 collective-permute-start.3
  33.8 2.4 collective-permute-start.2
  36.6 6.0 %scatter_custom_fusion = f32[10,64]{0,1:T(8,128)S(1)} fusion(s32[1024]{0:T(1024)S(1)} %bitcast.205, f32[1024,10]{1,0:T(8,128)S(1)} %copy.676, f32[]{:T(128)} %constant.342.clone.1), kind=kCustom, calls=%fused_computation.929 | custom fusion | flops 10240 | bytes 2564 | tf_op jit(solution)/shard_map/scatter-add | solution.py:86
  46.1 5.1 %collective-permute-start.9 = (f32[2,4,8,320]{3,2,1,0:T(8,128)S(1)}, f32[2,4,8,320]{3,2,1,0:T(8,128)S(1)}, u32[]{:S(2)}, u32[]{:S(2)}) collective-permute-start(f32[2,4,8,320]{3,2,1,0:T(8,128)S(1)} %get-tuple-element.249), channel_id=1, source_target_pairs={{4,0},{8,4},{12,8},{5,1},{9,5},{13,9},{6,2},{10,6},{14,10},{7,3},{... | collective-permute-start | bytes 245768 | tf_op jit(solution)/shard_map/ppermute | solution.py:17
  51.3 1.9 collective-permute-start.8
  53.4 4.3 %collective-permute-done.8 = f32[2,4,8,320]{3,2,1,0:T(8,128)S(1)} collective-permute-done((f32[2,4,8,320]{3,2,1,0:T(8,128)S(1)}, f32[2,4,8,320]{3,2,1,0:T(8,128)S(1)}, u32[]{:S(2)}, u32[]{:S(2)}) %collective-permute-start.8) | collective-permute-done | bytes 81952 | tf_op jit(solution)/shard_map/ppermute | solution.py:14
  57.9 1.9 collective-permute-start.11
  59.8 2.4 collective-permute-start.10
  63.1 3.8 %collective-permute-done.10 = f32[2,16,4,320]{3,1,2,0:T(8,128)S(1)} collective-permute-done((f32[2,16,4,320]{3,1,2,0:T(8,128)S(1)}, f32[2,16,4,320]{3,1,2,0:T(8,128)S(1)}, u32[]{:S(2)}, u32[]{:S(2)}) %collective-permute-start.10) | collective-permute-done | bytes 163872 | tf_op jit(solution)/shard_map/ppermute | solution.py:14
  68.5 2.0 collective-permute-start.13
  70.5 3.8 %collective-permute-start.12 = (f32[2,4,8,320]{3,2,1,0:T(8,128)S(1)}, f32[2,4,8,320]{3,2,1,0:T(8,128)S(1)}, u32[]{:S(2)}, u32[]{:S(2)}) collective-permute-start(f32[2,4,8,320]{3,2,1,0:T(8,128)S(1)} %get-tuple-element.246), channel_id=1, source_target_pairs={{0,4},{4,8},{8,12},{1,5},{5,9},{9,13},{2,6},{6,10},{10,14},{3,7},{... | collective-permute-start | bytes 245768 | tf_op jit(solution)/shard_map/ppermute | solution.py:14
  75.0 2.0 collective-permute-done.12
  77.1 1.9 collective-permute-start.15
  79.1 2.4 collective-permute-start.14
  82.3 3.8 %collective-permute-done.14 = f32[2,16,4,320]{3,1,2,0:T(8,128)S(1)} collective-permute-done((f32[2,16,4,320]{3,1,2,0:T(8,128)S(1)}, f32[2,16,4,320]{3,1,2,0:T(8,128)S(1)}, u32[]{:S(2)}, u32[]{:S(2)}) %collective-permute-start.14) | collective-permute-done | bytes 163872 | tf_op jit(solution)/shard_map/ppermute | solution.py:14
  87.8 1.9 collective-permute-start.17
  89.7 3.9 %collective-permute-start.16 = (f32[2,4,8,320]{3,2,1,0:T(8,128)S(1)}, f32[2,4,8,320]{3,2,1,0:T(8,128)S(1)}, u32[]{:S(2)}, u32[]{:S(2)}) collective-permute-start(f32[2,4,8,320]{3,2,1,0:T(8,128)S(1)} %get-tuple-element.244), channel_id=1, source_target_pairs={{0,4},{4,8},{8,12},{1,5},{5,9},{9,13},{2,6},{6,10},{10,14},{3,7},{... | collective-permute-start | bytes 245768 | tf_op jit(solution)/shard_map/ppermute | solution.py:14
  94.3 1.9 collective-permute-done.16
  96.4 1.9 collective-permute-start.19
  98.3 2.4 collective-permute-start.18
  101.6 3.8 %collective-permute-done.18 = f32[2,16,4,320]{3,1,2,0:T(8,128)S(1)} collective-permute-done((f32[2,16,4,320]{3,1,2,0:T(8,128)S(1)}, f32[2,16,4,320]{3,1,2,0:T(8,128)S(1)}, u32[]{:S(2)}, u32[]{:S(2)}) %collective-permute-start.18) | collective-permute-done | bytes 163872 | tf_op jit(solution)/shard_map/ppermute | solution.py:14
  107.1 1.9 collective-permute-start.21
  109.0 3.9 %collective-permute-start.20 = (f32[2,4,8,320]{3,2,1,0:T(8,128)S(1)}, f32[2,4,8,320]{3,2,1,0:T(8,128)S(1)}, u32[]{:S(2)}, u32[]{:S(2)}) collective-permute-start(f32[2,4,8,320]{3,2,1,0:T(8,128)S(1)} %get-tuple-element.242), channel_id=1, source_target_pairs={{0,4},{4,8},{8,12},{1,5},{5,9},{9,13},{2,6},{6,10},{10,14},{3,7},{... | collective-permute-start | bytes 245768 | tf_op jit(solution)/shard_map/ppermute | solution.py:14
  113.6 1.9 collective-permute-done.20
  115.6 1.9 collective-permute-start.23
  117.6 2.4 collective-permute-start.22
  120.8 3.8 %collective-permute-done.22 = f32[2,16,4,320]{3,1,2,0:T(8,128)S(1)} collective-permute-done((f32[2,16,4,320]{3,1,2,0:T(8,128)S(1)}, f32[2,16,4,320]{3,1,2,0:T(8,128)S(1)}, u32[]{:S(2)}, u32[]{:S(2)}) %collective-permute-start.22) | collective-permute-done | bytes 163872 | tf_op jit(solution)/shard_map/ppermute | solution.py:14
  126.3 1.9 collective-permute-start.25
  128.3 3.9 %collective-permute-start.24 = (f32[2,4,8,320]{3,2,1,0:T(8,128)S(1)}, f32[2,4,8,320]{3,2,1,0:T(8,128)S(1)}, u32[]{:S(2)}, u32[]{:S(2)}) collective-permute-start(f32[2,4,8,320]{3,2,1,0:T(8,128)S(1)} %get-tuple-element.240), channel_id=1, source_target_pairs={{0,4},{4,8},{8,12},{1,5},{5,9},{9,13},{2,6},{6,10},{10,14},{3,7},{... | collective-permute-start | bytes 245768 | tf_op jit(solution)/shard_map/ppermute | solution.py:14
  132.8 1.9 collective-permute-done.24
  134.9 1.9 collective-permute-start.27
  136.8 2.6 %collective-permute-start.26 = (f32[2,16,4,320]{3,1,2,0:T(8,128)S(1)}, f32[2,16,4,320]{3,1,2,0:T(8,128)S(1)}, u32[]{:S(2)}, u32[]{:S(2)}) collective-permute-start(f32[2,16,4,320]{3,1,2,0:T(8,128)S(1)} %copy.733), channel_id=1, source_target_pairs={{0,1},{1,2},{2,3},{4,5},{5,6},{6,7},{8,9},{9,10},{10,11},{12,13},{... | collective-permute-start | bytes 491528 | tf_op jit(solution)/shard_map/ppermute | solution.py:14
  140.1 3.8 %collective-permute-done.26 = f32[2,16,4,320]{3,1,2,0:T(8,128)S(1)} collective-permute-done((f32[2,16,4,320]{3,1,2,0:T(8,128)S(1)}, f32[2,16,4,320]{3,1,2,0:T(8,128)S(1)}, u32[]{:S(2)}, u32[]{:S(2)}) %collective-permute-start.26) | collective-permute-done | bytes 163872 | tf_op jit(solution)/shard_map/ppermute | solution.py:14
  145.6 1.9 collective-permute-start.29
  147.5 3.9 %collective-permute-start.28 = (f32[2,4,8,320]{3,2,1,0:T(8,128)S(1)}, f32[2,4,8,320]{3,2,1,0:T(8,128)S(1)}, u32[]{:S(2)}, u32[]{:S(2)}) collective-permute-start(f32[2,4,8,320]{3,2,1,0:T(8,128)S(1)} %get-tuple-element.238), channel_id=1, source_target_pairs={{0,4},{4,8},{8,12},{1,5},{5,9},{9,13},{2,6},{6,10},{10,14},{3,7},{... | collective-permute-start | bytes 245768 | tf_op jit(solution)/shard_map/ppermute | solution.py:14
  152.1 1.9 collective-permute-done.28
  154.2 1.9 collective-permute-start.31
  156.1 2.4 collective-permute-start.30
  159.3 3.8 %collective-permute-done.30 = f32[2,16,4,320]{3,1,2,0:T(8,128)S(1)} collective-permute-done((f32[2,16,4,320]{3,1,2,0:T(8,128)S(1)}, f32[2,16,4,320]{3,1,2,0:T(8,128)S(1)}, u32[]{:S(2)}, u32[]{:S(2)}) %collective-permute-start.30) | collective-permute-done | bytes 163872 | tf_op jit(solution)/shard_map/ppermute | solution.py:14
  164.9 1.9 collective-permute-start.33
  166.8 3.9 %collective-permute-start.32 = (f32[2,4,8,320]{3,2,1,0:T(8,128)S(1)}, f32[2,4,8,320]{3,2,1,0:T(8,128)S(1)}, u32[]{:S(2)}, u32[]{:S(2)}) collective-permute-start(f32[2,4,8,320]{3,2,1,0:T(8,128)S(1)} %get-tuple-element.236), channel_id=1, source_target_pairs={{0,4},{4,8},{8,12},{1,5},{5,9},{9,13},{2,6},{6,10},{10,14},{3,7},{... | collective-permute-start | bytes 245768 | tf_op jit(solution)/shard_map/ppermute | solution.py:14
  171.4 1.9 collective-permute-done.32
  173.4 1.9 collective-permute-start.35
  175.4 2.4 collective-permute-start.34
  178.6 3.8 %collective-permute-done.34 = f32[2,16,4,320]{3,1,2,0:T(8,128)S(1)} collective-permute-done((f32[2,16,4,320]{3,1,2,0:T(8,128)S(1)}, f32[2,16,4,320]{3,1,2,0:T(8,128)S(1)}, u32[]{:S(2)}, u32[]{:S(2)}) %collective-permute-start.34) | collective-permute-done | bytes 163872 | tf_op jit(solution)/shard_map/ppermute | solution.py:14
  184.1 1.9 collective-permute-start.37
  186.0 3.9 %collective-permute-start.36 = (f32[2,4,8,320]{3,2,1,0:T(8,128)S(1)}, f32[2,4,8,320]{3,2,1,0:T(8,128)S(1)}, u32[]{:S(2)}, u32[]{:S(2)}) collective-permute-start(f32[2,4,8,320]{3,2,1,0:T(8,128)S(1)} %get-tuple-element.234), channel_id=1, source_target_pairs={{0,4},{4,8},{8,12},{1,5},{5,9},{9,13},{2,6},{6,10},{10,14},{3,7},{... | collective-permute-start | bytes 245768 | tf_op jit(solution)/shard_map/ppermute | solution.py:14
  190.6 1.9 collective-permute-done.36
  192.7 1.9 collective-permute-start.39
  194.6 2.4 collective-permute-start.38
  197.8 3.8 %collective-permute-done.38 = f32[2,16,4,320]{3,1,2,0:T(8,128)S(1)} collective-permute-done((f32[2,16,4,320]{3,1,2,0:T(8,128)S(1)}, f32[2,16,4,320]{3,1,2,0:T(8,128)S(1)}, u32[]{:S(2)}, u32[]{:S(2)}) %collective-permute-start.38) | collective-permute-done | bytes 163872 | tf_op jit(solution)/shard_map/ppermute | solution.py:14
  203.4 2.1 collective-permute-start.41
  205.4 3.9 %collective-permute-start.40 = (f32[2,4,8,320]{3,2,1,0:T(8,128)S(1)}, f32[2,4,8,320]{3,2,1,0:T(8,128)S(1)}, u32[]{:S(2)}, u32[]{:S(2)}) collective-permute-start(f32[2,4,8,320]{3,2,1,0:T(8,128)S(1)} %get-tuple-element.232), channel_id=1, source_target_pairs={{0,4},{4,8},{8,12},{1,5},{5,9},{9,13},{2,6},{6,10},{10,14},{3,7},{... | collective-permute-start | bytes 245768 | tf_op jit(solution)/shard_map/ppermute | solution.py:14
  229.1 1.9 collective-permute-start.43
  231.1 2.4 collective-permute-start.42
  234.4 3.6 %collective-permute-done.42 = f32[2,16,4,320]{3,1,2,0:T(8,128)S(1)} collective-permute-done((f32[2,16,4,320]{3,1,2,0:T(8,128)S(1)}, f32[2,16,4,320]{3,1,2,0:T(8,128)S(1)}, u32[]{:S(2)}, u32[]{:S(2)}) %collective-permute-start.42) | collective-permute-done | bytes 163872 | tf_op jit(solution)/shard_map/ppermute | solution.py:14
  238.8 1.6 fusion.407
  241.3 7.0 %fusion.361 = (f32[8,8,320]{2,1,0:T(8,128)}, f32[8,8,320]{2,1,0:T(8,128)}) fusion(f32[8,8,320]{2,1,0:T(8,128)S(1)} %multiply_add_fusion.1, f32[8,8,320]{2,1,0:T(8,128)S(1)} %multiply_add_fusion.3, f32[8,8,320]{2,1,0:T(8,128)S(1)} %multiply_add_fusion.4, f32[8,8,320]{2,1,0:T(8,128)S(1)} %multiply_add_fusion.8, f32[8,8,320]{2,1,0:T(8,128)S(1)} %copy-done.8, ...), kind=kLoop, calls=%fused_computation.864 | loop fusion | flops 1228800 | bytes 1556530 | tf_op jit(solution)/shard_map/add | solution.py:124
  (211 shorter events, 39.0 us)
Async XLA Ops:
  0.6 6.8 %copy-start.6 = (f32[10,64]{1,0:T(8,128)S(1)}, f32[10,64]{1,0:T(8,128)}, u32[]{:S(2)}) copy-start(f32[10,64]{1,0:T(8,128)} %param.39) | copy-start | bytes 7684
  1.5 30.2 %collective-permute-start.1 = (f32[2,4,8,320]{3,2,1,0:T(8,128)S(1)}, f32[2,4,8,320]{3,2,1,0:T(8,128)S(1)}, u32[]{:S(2)}, u32[]{:S(2)}) collective-permute-start(f32[2,4,8,320]{3,2,1,0:T(8,128)S(1)} %get-tuple-element.251), channel_id=1, source_target_pairs={{4,0},{8,4},{12,8},{5,1},{9,5},{13,9},{6,2},{10,6},{14,10},{7,3},{... | collective-permute-start | bytes 245768 | tf_op jit(solution)/shard_map/ppermute | solution.py:17
  3.9 27.8 %collective-permute-start = (f32[2,4,8,320]{3,2,1,0:T(8,128)S(1)}, f32[2,4,8,320]{3,2,1,0:T(8,128)S(1)}, u32[]{:S(2)}, u32[]{:S(2)}) collective-permute-start(f32[2,4,8,320]{3,2,1,0:T(8,128)S(1)} %get-tuple-element.250), channel_id=1, source_target_pairs={{0,4},{4,8},{8,12},{1,5},{5,9},{9,13},{2,6},{6,10},{10,14},{3,7},{... | collective-permute-start | bytes 245768 | tf_op jit(solution)/shard_map/ppermute | solution.py:14
  7.4 12.3 %collective-permute-start.4 = (f32[10,64]{1,0:T(8,128)S(1)}, f32[10,64]{1,0:T(8,128)S(1)}, u32[]{:S(2)}, u32[]{:S(2)}) collective-permute-start(f32[10,64]{1,0:T(8,128)S(1)} %copy-done.6), channel_id=1, source_target_pairs={{0,15},{1,0},{2,1},{3,2},{4,3},{5,4},{6,5},{7,6},{8,7},{9,8},{10,9... | collective-permute-start | bytes 7688 | tf_op jit(solution)/shard_map/ppermute | solution.py:72
  8.2 0.7 copy-start.13
  8.2 17.8 %copy-start.10 = (f32[10]{0:T(128)S(1)}, f32[10]{0:T(128)}, u32[]{:S(2)}) copy-start(f32[10]{0:T(128)} %param.37) | copy-start | bytes 124
  8.8 1.3 copy-start.12
  10.1 21.6 %copy-start.1 = (f32[8,8,320]{2,1,0:T(8,128)S(1)}, f32[8,8,320]{2,1,0:T(8,128)}, u32[]{:S(2)}) copy-start(f32[8,8,320]{2,1,0:T(8,128)} %param.33) | copy-start | bytes 245764
  10.1 21.6 %copy-start.4 = (f32[8,8,320]{2,1,0:T(8,128)S(1)}, f32[8,8,320]{2,1,0:T(8,128)}, u32[]{:S(2)}) copy-start(f32[8,8,320]{2,1,0:T(8,128)} %param.35) | copy-start | bytes 245764
  19.8 4.6 %collective-permute-start.5 = (f32[10,128]{1,0:T(8,128)S(1)}, f32[10,128]{1,0:T(8,128)S(1)}, u32[]{:S(2)}, u32[]{:S(2)}) collective-permute-start(f32[10,128]{1,0:T(8,128)S(1)} %pad_maximum_fusion.32), channel_id=1, source_target_pairs={{0,14},{1,15},{2,0},{3,1},{4,2},{5,3},{6,4},{7,5},{8,6},{9,7},{10,... | collective-permute-start | bytes 15368 | tf_op jit(solution)/shard_map/ppermute | solution.py:72
  24.4 5.3 %collective-permute-start.6 = (f32[10,256]{1,0:T(8,128)S(1)}, f32[10,256]{1,0:T(8,128)S(1)}, u32[]{:S(2)}, u32[]{:S(2)}) collective-permute-start(f32[10,256]{1,0:T(8,128)S(1)} %pad_maximum_fusion.31), channel_id=1, source_target_pairs={{0,12},{1,13},{2,14},{3,15},{4,0},{5,1},{6,2},{7,3},{8,4},{9,5},{1... | collective-permute-start | bytes 30728 | tf_op jit(solution)/shard_map/ppermute | solution.py:72
  29.7 6.5 %collective-permute-start.7 = (f32[10,512]{1,0:T(8,128)S(1)}, f32[10,512]{1,0:T(8,128)S(1)}, u32[]{:S(2)}, u32[]{:S(2)}) collective-permute-start(f32[10,512]{1,0:T(8,128)S(1)} %pad_maximum_fusion.30), channel_id=1, source_target_pairs={{0,8},{1,9},{2,10},{3,11},{4,12},{5,13},{6,14},{7,15},{8,0},{9,1},... | collective-permute-start | bytes 61448 | tf_op jit(solution)/shard_map/ppermute | solution.py:72
  31.8 10.9 %collective-permute-start.3 = (f32[2,16,4,320]{3,1,2,0:T(8,128)S(1)}, f32[2,16,4,320]{3,1,2,0:T(8,128)S(1)}, u32[]{:S(2)}, u32[]{:S(2)}) collective-permute-start(f32[2,16,4,320]{3,1,2,0:T(8,128)S(1)} %copy.724), channel_id=1, source_target_pairs={{1,0},{2,1},{3,2},{5,4},{6,5},{7,6},{9,8},{10,9},{11,10},{13,12},{... | collective-permute-start | bytes 491528 | tf_op jit(solution)/shard_map/ppermute | solution.py:17
  33.8 9.0 %collective-permute-start.2 = (f32[2,16,4,320]{3,1,2,0:T(8,128)S(1)}, f32[2,16,4,320]{3,1,2,0:T(8,128)S(1)}, u32[]{:S(2)}, u32[]{:S(2)}) collective-permute-start(f32[2,16,4,320]{3,1,2,0:T(8,128)S(1)} %copy.723), channel_id=1, source_target_pairs={{0,1},{1,2},{2,3},{4,5},{5,6},{6,7},{8,9},{9,10},{10,11},{12,13},{... | collective-permute-start | bytes 491528 | tf_op jit(solution)/shard_map/ppermute | solution.py:14
  43.1 0.9 copy-start.9
  43.4 0.9 copy-start
  44.3 0.9 copy-start.7
  46.1 7.3 %collective-permute-start.9 = (f32[2,4,8,320]{3,2,1,0:T(8,128)S(1)}, f32[2,4,8,320]{3,2,1,0:T(8,128)S(1)}, u32[]{:S(2)}, u32[]{:S(2)}) collective-permute-start(f32[2,4,8,320]{3,2,1,0:T(8,128)S(1)} %get-tuple-element.249), channel_id=1, source_target_pairs={{4,0},{8,4},{12,8},{5,1},{9,5},{13,9},{6,2},{10,6},{14,10},{7,3},{... | collective-permute-start | bytes 245768 | tf_op jit(solution)/shard_map/ppermute | solution.py:17
  51.3 6.5 %collective-permute-start.8 = (f32[2,4,8,320]{3,2,1,0:T(8,128)S(1)}, f32[2,4,8,320]{3,2,1,0:T(8,128)S(1)}, u32[]{:S(2)}, u32[]{:S(2)}) collective-permute-start(f32[2,4,8,320]{3,2,1,0:T(8,128)S(1)} %get-tuple-element.248), channel_id=1, source_target_pairs={{0,4},{4,8},{8,12},{1,5},{5,9},{9,13},{2,6},{6,10},{10,14},{3,7},{... | collective-permute-start | bytes 245768 | tf_op jit(solution)/shard_map/ppermute | solution.py:14
  57.9 5.1 %collective-permute-start.11 = (f32[2,16,4,320]{3,1,2,0:T(8,128)S(1)}, f32[2,16,4,320]{3,1,2,0:T(8,128)S(1)}, u32[]{:S(2)}, u32[]{:S(2)}) collective-permute-start(f32[2,16,4,320]{3,1,2,0:T(8,128)S(1)} %copy.726), channel_id=1, source_target_pairs={{1,0},{2,1},{3,2},{5,4},{6,5},{7,6},{9,8},{10,9},{11,10},{13,12},{... | collective-permute-start | bytes 491528 | tf_op jit(solution)/shard_map/ppermute | solution.py:17
  59.8 7.0 %collective-permute-start.10 = (f32[2,16,4,320]{3,1,2,0:T(8,128)S(1)}, f32[2,16,4,320]{3,1,2,0:T(8,128)S(1)}, u32[]{:S(2)}, u32[]{:S(2)}) collective-permute-start(f32[2,16,4,320]{3,1,2,0:T(8,128)S(1)} %copy.725), channel_id=1, source_target_pairs={{0,1},{1,2},{2,3},{4,5},{5,6},{6,7},{8,9},{9,10},{10,11},{12,13},{... | collective-permute-start | bytes 491528 | tf_op jit(solution)/shard_map/ppermute | solution.py:14
  68.5 6.5 %collective-permute-start.13 = (f32[2,4,8,320]{3,2,1,0:T(8,128)S(1)}, f32[2,4,8,320]{3,2,1,0:T(8,128)S(1)}, u32[]{:S(2)}, u32[]{:S(2)}) collective-permute-start(f32[2,4,8,320]{3,2,1,0:T(8,128)S(1)} %get-tuple-element.247), channel_id=1, source_target_pairs={{4,0},{8,4},{12,8},{5,1},{9,5},{13,9},{6,2},{10,6},{14,10},{7,3},{... | collective-permute-start | bytes 245768 | tf_op jit(solution)/shard_map/ppermute | solution.py:17
  70.5 6.5 %collective-permute-start.12 = (f32[2,4,8,320]{3,2,1,0:T(8,128)S(1)}, f32[2,4,8,320]{3,2,1,0:T(8,128)S(1)}, u32[]{:S(2)}, u32[]{:S(2)}) collective-permute-start(f32[2,4,8,320]{3,2,1,0:T(8,128)S(1)} %get-tuple-element.246), channel_id=1, source_target_pairs={{0,4},{4,8},{8,12},{1,5},{5,9},{9,13},{2,6},{6,10},{10,14},{3,7},{... | collective-permute-start | bytes 245768 | tf_op jit(solution)/shard_map/ppermute | solution.py:14
  77.1 5.1 %collective-permute-start.15 = (f32[2,16,4,320]{3,1,2,0:T(8,128)S(1)}, f32[2,16,4,320]{3,1,2,0:T(8,128)S(1)}, u32[]{:S(2)}, u32[]{:S(2)}) collective-permute-start(f32[2,16,4,320]{3,1,2,0:T(8,128)S(1)} %copy.728), channel_id=1, source_target_pairs={{1,0},{2,1},{3,2},{5,4},{6,5},{7,6},{9,8},{10,9},{11,10},{13,12},{... | collective-permute-start | bytes 491528 | tf_op jit(solution)/shard_map/ppermute | solution.py:17
  79.1 7.0 %collective-permute-start.14 = (f32[2,16,4,320]{3,1,2,0:T(8,128)S(1)}, f32[2,16,4,320]{3,1,2,0:T(8,128)S(1)}, u32[]{:S(2)}, u32[]{:S(2)}) collective-permute-start(f32[2,16,4,320]{3,1,2,0:T(8,128)S(1)} %copy.727), channel_id=1, source_target_pairs={{0,1},{1,2},{2,3},{4,5},{5,6},{6,7},{8,9},{9,10},{10,11},{12,13},{... | collective-permute-start | bytes 491528 | tf_op jit(solution)/shard_map/ppermute | solution.py:14
  87.8 6.5 %collective-permute-start.17 = (f32[2,4,8,320]{3,2,1,0:T(8,128)S(1)}, f32[2,4,8,320]{3,2,1,0:T(8,128)S(1)}, u32[]{:S(2)}, u32[]{:S(2)}) collective-permute-start(f32[2,4,8,320]{3,2,1,0:T(8,128)S(1)} %get-tuple-element.245), channel_id=1, source_target_pairs={{4,0},{8,4},{12,8},{5,1},{9,5},{13,9},{6,2},{10,6},{14,10},{7,3},{... | collective-permute-start | bytes 245768 | tf_op jit(solution)/shard_map/ppermute | solution.py:17
  89.7 6.5 %collective-permute-start.16 = (f32[2,4,8,320]{3,2,1,0:T(8,128)S(1)}, f32[2,4,8,320]{3,2,1,0:T(8,128)S(1)}, u32[]{:S(2)}, u32[]{:S(2)}) collective-permute-start(f32[2,4,8,320]{3,2,1,0:T(8,128)S(1)} %get-tuple-element.244), channel_id=1, source_target_pairs={{0,4},{4,8},{8,12},{1,5},{5,9},{9,13},{2,6},{6,10},{10,14},{3,7},{... | collective-permute-start | bytes 245768 | tf_op jit(solution)/shard_map/ppermute | solution.py:14
  96.4 5.1 %collective-permute-start.19 = (f32[2,16,4,320]{3,1,2,0:T(8,128)S(1)}, f32[2,16,4,320]{3,1,2,0:T(8,128)S(1)}, u32[]{:S(2)}, u32[]{:S(2)}) collective-permute-start(f32[2,16,4,320]{3,1,2,0:T(8,128)S(1)} %copy.730), channel_id=1, source_target_pairs={{1,0},{2,1},{3,2},{5,4},{6,5},{7,6},{9,8},{10,9},{11,10},{13,12},{... | collective-permute-start | bytes 491528 | tf_op jit(solution)/shard_map/ppermute | solution.py:17
  98.3 7.0 %collective-permute-start.18 = (f32[2,16,4,320]{3,1,2,0:T(8,128)S(1)}, f32[2,16,4,320]{3,1,2,0:T(8,128)S(1)}, u32[]{:S(2)}, u32[]{:S(2)}) collective-permute-start(f32[2,16,4,320]{3,1,2,0:T(8,128)S(1)} %copy.729), channel_id=1, source_target_pairs={{0,1},{1,2},{2,3},{4,5},{5,6},{6,7},{8,9},{9,10},{10,11},{12,13},{... | collective-permute-start | bytes 491528 | tf_op jit(solution)/shard_map/ppermute | solution.py:14
  107.1 6.5 %collective-permute-start.21 = (f32[2,4,8,320]{3,2,1,0:T(8,128)S(1)}, f32[2,4,8,320]{3,2,1,0:T(8,128)S(1)}, u32[]{:S(2)}, u32[]{:S(2)}) collective-permute-start(f32[2,4,8,320]{3,2,1,0:T(8,128)S(1)} %get-tuple-element.243), channel_id=1, source_target_pairs={{4,0},{8,4},{12,8},{5,1},{9,5},{13,9},{6,2},{10,6},{14,10},{7,3},{... | collective-permute-start | bytes 245768 | tf_op jit(solution)/shard_map/ppermute | solution.py:17
  109.0 6.5 %collective-permute-start.20 = (f32[2,4,8,320]{3,2,1,0:T(8,128)S(1)}, f32[2,4,8,320]{3,2,1,0:T(8,128)S(1)}, u32[]{:S(2)}, u32[]{:S(2)}) collective-permute-start(f32[2,4,8,320]{3,2,1,0:T(8,128)S(1)} %get-tuple-element.242), channel_id=1, source_target_pairs={{0,4},{4,8},{8,12},{1,5},{5,9},{9,13},{2,6},{6,10},{10,14},{3,7},{... | collective-permute-start | bytes 245768 | tf_op jit(solution)/shard_map/ppermute | solution.py:14
  115.6 5.1 %collective-permute-start.23 = (f32[2,16,4,320]{3,1,2,0:T(8,128)S(1)}, f32[2,16,4,320]{3,1,2,0:T(8,128)S(1)}, u32[]{:S(2)}, u32[]{:S(2)}) collective-permute-start(f32[2,16,4,320]{3,1,2,0:T(8,128)S(1)} %copy.732), channel_id=1, source_target_pairs={{1,0},{2,1},{3,2},{5,4},{6,5},{7,6},{9,8},{10,9},{11,10},{13,12},{... | collective-permute-start | bytes 491528 | tf_op jit(solution)/shard_map/ppermute | solution.py:17
  117.6 7.0 %collective-permute-start.22 = (f32[2,16,4,320]{3,1,2,0:T(8,128)S(1)}, f32[2,16,4,320]{3,1,2,0:T(8,128)S(1)}, u32[]{:S(2)}, u32[]{:S(2)}) collective-permute-start(f32[2,16,4,320]{3,1,2,0:T(8,128)S(1)} %copy.731), channel_id=1, source_target_pairs={{0,1},{1,2},{2,3},{4,5},{5,6},{6,7},{8,9},{9,10},{10,11},{12,13},{... | collective-permute-start | bytes 491528 | tf_op jit(solution)/shard_map/ppermute | solution.py:14
  126.3 6.5 %collective-permute-start.25 = (f32[2,4,8,320]{3,2,1,0:T(8,128)S(1)}, f32[2,4,8,320]{3,2,1,0:T(8,128)S(1)}, u32[]{:S(2)}, u32[]{:S(2)}) collective-permute-start(f32[2,4,8,320]{3,2,1,0:T(8,128)S(1)} %get-tuple-element.241), channel_id=1, source_target_pairs={{4,0},{8,4},{12,8},{5,1},{9,5},{13,9},{6,2},{10,6},{14,10},{7,3},{... | collective-permute-start | bytes 245768 | tf_op jit(solution)/shard_map/ppermute | solution.py:17
  128.3 6.5 %collective-permute-start.24 = (f32[2,4,8,320]{3,2,1,0:T(8,128)S(1)}, f32[2,4,8,320]{3,2,1,0:T(8,128)S(1)}, u32[]{:S(2)}, u32[]{:S(2)}) collective-permute-start(f32[2,4,8,320]{3,2,1,0:T(8,128)S(1)} %get-tuple-element.240), channel_id=1, source_target_pairs={{0,4},{4,8},{8,12},{1,5},{5,9},{9,13},{2,6},{6,10},{10,14},{3,7},{... | collective-permute-start | bytes 245768 | tf_op jit(solution)/shard_map/ppermute | solution.py:14
  134.9 5.1 %collective-permute-start.27 = (f32[2,16,4,320]{3,1,2,0:T(8,128)S(1)}, f32[2,16,4,320]{3,1,2,0:T(8,128)S(1)}, u32[]{:S(2)}, u32[]{:S(2)}) collective-permute-start(f32[2,16,4,320]{3,1,2,0:T(8,128)S(1)} %copy.734), channel_id=1, source_target_pairs={{1,0},{2,1},{3,2},{5,4},{6,5},{7,6},{9,8},{10,9},{11,10},{13,12},{... | collective-permute-start | bytes 491528 | tf_op jit(solution)/shard_map/ppermute | solution.py:17
  136.8 7.0 %collective-permute-start.26 = (f32[2,16,4,320]{3,1,2,0:T(8,128)S(1)}, f32[2,16,4,320]{3,1,2,0:T(8,128)S(1)}, u32[]{:S(2)}, u32[]{:S(2)}) collective-permute-start(f32[2,16,4,320]{3,1,2,0:T(8,128)S(1)} %copy.733), channel_id=1, source_target_pairs={{0,1},{1,2},{2,3},{4,5},{5,6},{6,7},{8,9},{9,10},{10,11},{12,13},{... | collective-permute-start | bytes 491528 | tf_op jit(solution)/shard_map/ppermute | solution.py:14
  145.6 6.5 %collective-permute-start.29 = (f32[2,4,8,320]{3,2,1,0:T(8,128)S(1)}, f32[2,4,8,320]{3,2,1,0:T(8,128)S(1)}, u32[]{:S(2)}, u32[]{:S(2)}) collective-permute-start(f32[2,4,8,320]{3,2,1,0:T(8,128)S(1)} %get-tuple-element.239), channel_id=1, source_target_pairs={{4,0},{8,4},{12,8},{5,1},{9,5},{13,9},{6,2},{10,6},{14,10},{7,3},{... | collective-permute-start | bytes 245768 | tf_op jit(solution)/shard_map/ppermute | solution.py:17
  147.5 6.5 %collective-permute-start.28 = (f32[2,4,8,320]{3,2,1,0:T(8,128)S(1)}, f32[2,4,8,320]{3,2,1,0:T(8,128)S(1)}, u32[]{:S(2)}, u32[]{:S(2)}) collective-permute-start(f32[2,4,8,320]{3,2,1,0:T(8,128)S(1)} %get-tuple-element.238), channel_id=1, source_target_pairs={{0,4},{4,8},{8,12},{1,5},{5,9},{9,13},{2,6},{6,10},{10,14},{3,7},{... | collective-permute-start | bytes 245768 | tf_op jit(solution)/shard_map/ppermute | solution.py:14
  154.2 5.1 %collective-permute-start.31 = (f32[2,16,4,320]{3,1,2,0:T(8,128)S(1)}, f32[2,16,4,320]{3,1,2,0:T(8,128)S(1)}, u32[]{:S(2)}, u32[]{:S(2)}) collective-permute-start(f32[2,16,4,320]{3,1,2,0:T(8,128)S(1)} %copy.736), channel_id=1, source_target_pairs={{1,0},{2,1},{3,2},{5,4},{6,5},{7,6},{9,8},{10,9},{11,10},{13,12},{... | collective-permute-start | bytes 491528 | tf_op jit(solution)/shard_map/ppermute | solution.py:17
  156.1 7.0 %collective-permute-start.30 = (f32[2,16,4,320]{3,1,2,0:T(8,128)S(1)}, f32[2,16,4,320]{3,1,2,0:T(8,128)S(1)}, u32[]{:S(2)}, u32[]{:S(2)}) collective-permute-start(f32[2,16,4,320]{3,1,2,0:T(8,128)S(1)} %copy.735), channel_id=1, source_target_pairs={{0,1},{1,2},{2,3},{4,5},{5,6},{6,7},{8,9},{9,10},{10,11},{12,13},{... | collective-permute-start | bytes 491528 | tf_op jit(solution)/shard_map/ppermute | solution.py:14
  164.9 6.5 %collective-permute-start.33 = (f32[2,4,8,320]{3,2,1,0:T(8,128)S(1)}, f32[2,4,8,320]{3,2,1,0:T(8,128)S(1)}, u32[]{:S(2)}, u32[]{:S(2)}) collective-permute-start(f32[2,4,8,320]{3,2,1,0:T(8,128)S(1)} %get-tuple-element.237), channel_id=1, source_target_pairs={{4,0},{8,4},{12,8},{5,1},{9,5},{13,9},{6,2},{10,6},{14,10},{7,3},{... | collective-permute-start | bytes 245768 | tf_op jit(solution)/shard_map/ppermute | solution.py:17
  166.8 6.5 %collective-permute-start.32 = (f32[2,4,8,320]{3,2,1,0:T(8,128)S(1)}, f32[2,4,8,320]{3,2,1,0:T(8,128)S(1)}, u32[]{:S(2)}, u32[]{:S(2)}) collective-permute-start(f32[2,4,8,320]{3,2,1,0:T(8,128)S(1)} %get-tuple-element.236), channel_id=1, source_target_pairs={{0,4},{4,8},{8,12},{1,5},{5,9},{9,13},{2,6},{6,10},{10,14},{3,7},{... | collective-permute-start | bytes 245768 | tf_op jit(solution)/shard_map/ppermute | solution.py:14
  173.4 5.1 %collective-permute-start.35 = (f32[2,16,4,320]{3,1,2,0:T(8,128)S(1)}, f32[2,16,4,320]{3,1,2,0:T(8,128)S(1)}, u32[]{:S(2)}, u32[]{:S(2)}) collective-permute-start(f32[2,16,4,320]{3,1,2,0:T(8,128)S(1)} %copy.738), channel_id=1, source_target_pairs={{1,0},{2,1},{3,2},{5,4},{6,5},{7,6},{9,8},{10,9},{11,10},{13,12},{... | collective-permute-start | bytes 491528 | tf_op jit(solution)/shard_map/ppermute | solution.py:17
  175.4 7.0 %collective-permute-start.34 = (f32[2,16,4,320]{3,1,2,0:T(8,128)S(1)}, f32[2,16,4,320]{3,1,2,0:T(8,128)S(1)}, u32[]{:S(2)}, u32[]{:S(2)}) collective-permute-start(f32[2,16,4,320]{3,1,2,0:T(8,128)S(1)} %copy.737), channel_id=1, source_target_pairs={{0,1},{1,2},{2,3},{4,5},{5,6},{6,7},{8,9},{9,10},{10,11},{12,13},{... | collective-permute-start | bytes 491528 | tf_op jit(solution)/shard_map/ppermute | solution.py:14
  184.1 6.5 %collective-permute-start.37 = (f32[2,4,8,320]{3,2,1,0:T(8,128)S(1)}, f32[2,4,8,320]{3,2,1,0:T(8,128)S(1)}, u32[]{:S(2)}, u32[]{:S(2)}) collective-permute-start(f32[2,4,8,320]{3,2,1,0:T(8,128)S(1)} %get-tuple-element.235), channel_id=1, source_target_pairs={{4,0},{8,4},{12,8},{5,1},{9,5},{13,9},{6,2},{10,6},{14,10},{7,3},{... | collective-permute-start | bytes 245768 | tf_op jit(solution)/shard_map/ppermute | solution.py:17
  186.0 6.5 %collective-permute-start.36 = (f32[2,4,8,320]{3,2,1,0:T(8,128)S(1)}, f32[2,4,8,320]{3,2,1,0:T(8,128)S(1)}, u32[]{:S(2)}, u32[]{:S(2)}) collective-permute-start(f32[2,4,8,320]{3,2,1,0:T(8,128)S(1)} %get-tuple-element.234), channel_id=1, source_target_pairs={{0,4},{4,8},{8,12},{1,5},{5,9},{9,13},{2,6},{6,10},{10,14},{3,7},{... | collective-permute-start | bytes 245768 | tf_op jit(solution)/shard_map/ppermute | solution.py:14
  192.7 5.1 %collective-permute-start.39 = (f32[2,16,4,320]{3,1,2,0:T(8,128)S(1)}, f32[2,16,4,320]{3,1,2,0:T(8,128)S(1)}, u32[]{:S(2)}, u32[]{:S(2)}) collective-permute-start(f32[2,16,4,320]{3,1,2,0:T(8,128)S(1)} %copy.740), channel_id=1, source_target_pairs={{1,0},{2,1},{3,2},{5,4},{6,5},{7,6},{9,8},{10,9},{11,10},{13,12},{... | collective-permute-start | bytes 491528 | tf_op jit(solution)/shard_map/ppermute | solution.py:17
  194.6 7.0 %collective-permute-start.38 = (f32[2,16,4,320]{3,1,2,0:T(8,128)S(1)}, f32[2,16,4,320]{3,1,2,0:T(8,128)S(1)}, u32[]{:S(2)}, u32[]{:S(2)}) collective-permute-start(f32[2,16,4,320]{3,1,2,0:T(8,128)S(1)} %copy.739), channel_id=1, source_target_pairs={{0,1},{1,2},{2,3},{4,5},{5,6},{6,7},{8,9},{9,10},{10,11},{12,13},{... | collective-permute-start | bytes 491528 | tf_op jit(solution)/shard_map/ppermute | solution.py:14
  202.4 38.8 %copy-start.3 = (f32[8,8,320]{2,1,0:T(8,128)}, f32[8,8,320]{2,1,0:T(8,128)S(1)}, u32[]{:S(2)}) copy-start(f32[8,8,320]{2,1,0:T(8,128)S(1)} %multiply_add_fusion.1) | copy-start | bytes 245764
  203.3 35.5 %copy-start.2 = (f32[8,8,320]{2,1,0:T(8,128)}, f32[8,8,320]{2,1,0:T(8,128)S(1)}, u32[]{:S(2)}) copy-start(f32[8,8,320]{2,1,0:T(8,128)S(1)} %get-tuple-element.175) | copy-start | bytes 245764
  203.3 6.0 %copy-start.11 = (s32[4]{0:T(128)S(1)}, s32[4]{0:T(128)}, u32[]{:S(2)}) copy-start(s32[4]{0:T(128)} %param.41) | copy-start | bytes 52
  203.4 25.6 %collective-permute-start.41 = (f32[2,4,8,320]{3,2,1,0:T(8,128)S(1)}, f32[2,4,8,320]{3,2,1,0:T(8,128)S(1)}, u32[]{:S(2)}, u32[]{:S(2)}) collective-permute-start(f32[2,4,8,320]{3,2,1,0:T(8,128)S(1)} %get-tuple-element.233), channel_id=1, source_target_pairs={{4,0},{8,4},{12,8},{5,1},{9,5},{13,9},{6,2},{10,6},{14,10},{7,3},{... | collective-permute-start | bytes 245768 | tf_op jit(solution)/shard_map/ppermute | solution.py:17
  205.4 23.6 %collective-permute-start.40 = (f32[2,4,8,320]{3,2,1,0:T(8,128)S(1)}, f32[2,4,8,320]{3,2,1,0:T(8,128)S(1)}, u32[]{:S(2)}, u32[]{:S(2)}) collective-permute-start(f32[2,4,8,320]{3,2,1,0:T(8,128)S(1)} %get-tuple-element.232), channel_id=1, source_target_pairs={{0,4},{4,8},{8,12},{1,5},{5,9},{9,13},{2,6},{6,10},{10,14},{3,7},{... | collective-permute-start | bytes 245768 | tf_op jit(solution)/shard_map/ppermute | solution.py:14
  229.1 5.2 %collective-permute-start.43 = (f32[2,16,4,320]{3,1,2,0:T(8,128)S(1)}, f32[2,16,4,320]{3,1,2,0:T(8,128)S(1)}, u32[]{:S(2)}, u32[]{:S(2)}) collective-permute-start(f32[2,16,4,320]{3,1,2,0:T(8,128)S(1)} %copy.742), channel_id=1, source_target_pairs={{1,0},{2,1},{3,2},{5,4},{6,5},{7,6},{9,8},{10,9},{11,10},{13,12},{... | collective-permute-start | bytes 491528 | tf_op jit(solution)/shard_map/ppermute | solution.py:17
  231.1 7.0 %collective-permute-start.42 = (f32[2,16,4,320]{3,1,2,0:T(8,128)S(1)}, f32[2,16,4,320]{3,1,2,0:T(8,128)S(1)}, u32[]{:S(2)}, u32[]{:S(2)}) collective-permute-start(f32[2,16,4,320]{3,1,2,0:T(8,128)S(1)} %copy.741), channel_id=1, source_target_pairs={{0,1},{1,2},{2,3},{4,5},{5,6},{6,7},{8,9},{9,10},{10,11},{12,13},{... | collective-permute-start | bytes 491528 | tf_op jit(solution)/shard_map/ppermute | solution.py:14
  240.3 0.9 copy-start.5
  240.4 1.0 copy-start.8
